TPU v7x, 32 devices: a whole 2x2x4 slice. The times are simulated.
32 devices in a mesh: groups: 2 (over x), vid: 8 (over z, y), tok: 2 (over core).
Axes of the slice: x: 2, y: 2, z: 4, core: 2. Of those that a mesh axis runs over, the one named last changes fastest.
Arguments:
- captions: bfloat16 [16, 128, 32, 128], P(('groups', 'vid')), parts along dimension 0, may hold values from -8 to 8
- caption_lengths: int32 [16, 128], P(('groups', 'vid')), parts along dimension 0, may hold values from 1 to 32
- video_bank: bfloat16 [192, 256, 128], P(('groups', 'vid'), 'tok'), parts along dimension 0, may hold values from -1.5 to 1.5
- owner_order: int32 [6], P('groups'), parts along dimension 0, may hold values from 0 to 7, as said below
Outputs:
- scores: float32 [192, 384], P(('groups', 'vid')), parts along dimension 0
There are 2 independent parts, one for each index of `groups`. A program takes and returns all parts, laid end to end along the dimension named above; each array names one. Nothing has to cross between parts.
Inputs may be any that keep to these rules, and one draw needn't show every extreme that they name: `caption_lengths`: token slot j of a caption is real when j is less than its count. `owner_order`: 3 different block indices.
All inputs are finite; a program needn't handle non-finite values.
Results may differ from a plain program's by a relative error of at most 0.0003.
Values may be sent and summed in bfloat16 or wider, within the bound.
No kernel may reach another device: no remote copies, remote signals or barrier semaphores. Data moves between devices by JAX's collectives and lax.ppermute only.
A program may use at most 64 MiB of HBM per device.

v0:
```python
import jax
import jax.numpy as jnp
from jax import lax
from jax.sharding import PartitionSpec as P

ROUNDS = 3


sharpness_factor = 5.0


def spread(value, axis, source):
    kept = jnp.where(lax.axis_index(axis) == source, value, 0).astype(value.dtype)
    return lax.psum(kept, axis)


def mask_weights(counts, slot_count):
    slots = jnp.arange(slot_count, dtype=jnp.int32)
    lengths_float = counts.astype(jnp.float32)
    return (slots[None, :] < counts[:, None]).astype(jnp.float32) / lengths_float[:, None]


def per_device(captions, caption_lengths, video_bank, owner_order):
    results = []
    bank_whole = lax.all_gather(video_bank, "tok", axis=1, tiled=True)
    share_rows = captions.shape[1] // lax.axis_size("tok")
    start_row = lax.axis_index("tok") * share_rows
    for round_index in range(ROUNDS):
        owner_now = owner_order[round_index]
        my_share = lax.dynamic_slice_in_dim(captions[0], start_row, share_rows, 0)
        my_counts = lax.dynamic_slice_in_dim(caption_lengths[0], start_row, share_rows, 0)
        share_rows_now, share_counts = (
            spread(my_share, "vid", owner_now),
            spread(my_counts, "vid", owner_now),
        )
        slot_count = share_rows_now.shape[1]
        query_rows = share_rows_now.reshape(share_rows * slot_count, share_rows_now.shape[2])

        def whole_video(footage_key_matrix):
            raw_similarity = (
                lax.dot_general(
                    query_rows,
                    footage_key_matrix,
                    (((1,), (1,)), ((), ())),
                    preferred_element_type=jnp.float32,
                )
                * sharpness_factor
            )
            row_peak = jnp.max(raw_similarity, axis=1)
            row_accumulated = jnp.sum(jnp.exp(raw_similarity - row_peak[:, None]), axis=1)
            return (row_peak + jnp.log(row_accumulated)) / sharpness_factor

        smoothed_scores = lax.map(whole_video, bank_whole).reshape(
            video_bank.shape[0], share_rows, slot_count
        )
        weights = mask_weights(share_counts, slot_count)
        results.append(
            jnp.einsum("vcj,cj->vc", smoothed_scores, weights, precision=lax.Precision.HIGHEST)
        )
    stacked = jnp.stack(results, axis=1)
    gathered = lax.all_gather(stacked, "tok", axis=2, tiled=True)
    return gathered.reshape(video_bank.shape[0], ROUNDS * captions.shape[1])


def solution(mesh):
    return jax.shard_map(
        per_device,
        mesh=mesh,
        in_specs=(
            P(("groups", "vid"), None, None, None),
            P(("groups", "vid"), None),
            P(("groups", "vid"), "tok", None),
            P("groups"),
        ),
        out_specs=P(("groups", "vid"), None),
        check_vma=False,
    )
```

profile of v0, /device:TPU:0, one launch (start us, length us, event | category | flops | bytes accessed | tf_op | source)
XLA Modules:
  0.0 167.1 jit_solution(8382262049726424937)
XLA Ops:
  6.5 1.4 fusion.21
  9.9 2.3 %broadcast_select_fusion.2 = (bf16[1,64,32,128]{3,2,1,0:T(8,128)(2,1)}, bf16[1,64,32,128]{3,2,1,0:T(8,128)(2,1)}, bf16[1,64,32,128]{3,2,1,0:T(8,128)(2,1)}) fusion(pred[]{:T(512)S(6)} %eq.12, bf16[1,128,32,128]{3,2,1,0:T(8,128)(2,1)} %param.10, s32[]{:T(128)S(6)} %select_n.67, pred[]{:T(512)S(6)} %eq.13, pred[]{:T(512)S(6)} %eq.14), kind=kLoop, calls=%fused_computation.26 | loop fusion | flops 786432 | bytes 2097159 | tf_op jit(solution)/shard_map/jit(_where)/select_n | solution.py:13
  12.3 13.5 %all-reduce = (s32[64]{0:T(128)S(1)}, s32[64]{0:T(128)S(1)}, s32[64]{0:T(128)S(1)}) all-reduce(s32[64]{0:T(128)S(1)} %get-tuple-element.115, s32[64]{0:T(128)S(1)} %get-tuple-element.114, s32[64]{0:T(128)S(1)} %get-tuple-element.113), channel_id=1, replica_groups=mesh['groups'=2,'vid'=8,'tok'=2] {'vid'}, use_global_device_ids=true, to_apply=%region_12.13 | all-reduce | flops 192 | bytes 1536 | tf_op jit(solution)/shard_map/psum | solution.py:14
  25.8 2.4 %all_gather.6 = bf16[12,256,128]{2,1,0:T(8,128)(2,1)S(1)} all-gather(bf16[12,128,128]{2,1,0:T(8,128)(2,1)S(1)} %copy-done.2), channel_id=1, replica_groups=mesh['groups'=2,'vid'=8,'tok'=2] {'tok'}, dimensions={1}, use_global_device_ids=true | all-gather | bytes 1179648 | tf_op jit(solution)/shard_map/all_gather | solution.py:25
  28.4 76.2 %all-reduce.4.cloned.1.call-done = (bf16[2048,128]{1,0:T(8,128)(2,1)}, bf16[2048,128]{1,0:T(8,128)(2,1)}, bf16[2048,128]{1,0:T(8,128)(2,1)}) async-done(((bf16[2048,128]{1,0:T(8,128)(2,1)}, bf16[2048,128]{1,0:T(8,128)(2,1)}, bf16[2048,128]{1,0:T(8,128)(2,1)}), (bf16[2048,128]{1,0:T(8,128)(2,1)}, bf16[2048,128]{1,0:T(8,128)(2,1)}, bf16[2048,128]{1,0:T(8,128)(2,1)})) %all-reduce.4.cloned.1.call-update) | async-done | bytes 1572880 | tf_op jit(solution)/shard_map/psum | solution.py:14
  104.6 24.6 %while.30 = (s32[]{:T(128)}, f32[12,2048]{1,0:T(8,128)S(1)}, bf16[12,256,128]{2,1,0:T(8,128)(2,1)S(1)}, bf16[2048,128]{1,0:T(8,128)(2,1)}, s32[]{:T(128)}, /*index=5*/s32[]{:T(128)}) while((s32[]{:T(128)}, f32[12,2048]{1,0:T(8,128)S(1)}, bf16[12,256,128]{2,1,0:T(8,128)(2,1)S(1)}, bf16[2048,128]{1,0:T(8,128)(2,1)}, s32[]{:T(128)}, ...), condition=%wide.region_5.6_spmd, body=%wide.region_2.5_spmd.sunk | while | flops 136314880 | bytes 4849741 | solution.py:53
  104.6 1.5 fusion.35
  106.2 0.3 exponential_reduce_fusion.6
  106.7 1.5 fusion.35
  108.2 0.3 exponential_reduce_fusion.6
  108.8 1.5 fusion.35
  110.3 0.3 exponential_reduce_fusion.6
  110.8 1.5 fusion.35
  112.9 1.5 fusion.35
  114.9 1.5 fusion.35
  117.0 1.5 fusion.35
  119.0 1.5 fusion.35
  121.1 1.5 fusion.35
  123.1 1.5 fusion.35
  125.2 1.5 fusion.35
  127.2 1.5 fusion.35
  129.4 1.1 fusion.13
  130.6 12.0 %while.31 = (s32[]{:T(128)}, f32[12,2048]{1,0:T(8,128)S(1)}, bf16[12,256,128]{2,1,0:T(8,128)(2,1)S(1)}, bf16[2048,128]{1,0:T(8,128)(2,1)S(1)}, s32[]{:T(128)}, /*index=5*/s32[]{:T(128)}) while((s32[]{:T(128)}, f32[12,2048]{1,0:T(8,128)S(1)}, bf16[12,256,128]{2,1,0:T(8,128)(2,1)S(1)}, bf16[2048,128]{1,0:T(8,128)(2,1)S(1)}, s32[]{:T(128)}, ...), condition=%wide.region_11.12_spmd, body=%wide.region_8.11_spmd.sunk | while | flops 136314880 | bytes 4849741 | solution.py:53
  130.6 0.4 fusion.37
  131.6 0.4 fusion.37
  132.6 0.4 fusion.37
  133.6 0.4 fusion.37
  134.6 0.4 fusion.37
  135.7 0.4 fusion.37
  136.7 0.4 fusion.37
  137.7 0.4 fusion.37
  138.7 0.4 fusion.37
  139.7 0.4 fusion.37
  140.7 0.4 fusion.37
  141.7 0.4 fusion.37
  142.8 1.1 fusion.11
  144.0 12.0 %while.32 = (s32[]{:T(128)}, f32[12,2048]{1,0:T(8,128)S(1)}, bf16[12,256,128]{2,1,0:T(8,128)(2,1)S(1)}, bf16[2048,128]{1,0:T(8,128)(2,1)S(1)}, s32[]{:T(128)}, /*index=5*/s32[]{:T(128)}) while((s32[]{:T(128)}, f32[12,2048]{1,0:T(8,128)S(1)}, bf16[12,256,128]{2,1,0:T(8,128)(2,1)S(1)}, bf16[2048,128]{1,0:T(8,128)(2,1)S(1)}, s32[]{:T(128)}, ...), condition=%wide.region_17.18_spmd, body=%wide.region_14.17_spmd.sunk | while | flops 136314880 | bytes 4849741 | solution.py:53
  144.0 0.4 fusion.39
  144.5 0.3 exponential_reduce_fusion.8
  145.0 0.4 fusion.39
  145.5 0.3 exponential_reduce_fusion.8
  146.0 0.4 fusion.39
  146.5 0.3 exponential_reduce_fusion.8
  147.1 0.4 fusion.39
  147.5 0.3 exponential_reduce_fusion.8
  148.1 0.4 fusion.39
  148.5 0.3 exponential_reduce_fusion.8
  149.1 0.4 fusion.39
  149.5 0.3 exponential_reduce_fusion.8
  150.1 0.4 fusion.39
  150.5 0.3 exponential_reduce_fusion.8
  151.1 0.4 fusion.39
  151.5 0.3 exponential_reduce_fusion.8
  152.1 0.4 fusion.39
  152.5 0.3 exponential_reduce_fusion.8
  153.1 0.4 fusion.39
  153.5 0.3 exponential_reduce_fusion.8
  154.1 0.4 fusion.39
  154.5 0.3 exponential_reduce_fusion.8
  155.1 0.4 fusion.39
  155.5 0.3 exponential_reduce_fusion.8
  156.2 1.1 fusion.9
  157.6 2.0 %all_gather.7 = f32[12,3,128]{0,1,2:T(4,128)S(1)} all-gather(f32[12,3,64]{0,1,2:T(4,128)S(1)} %copy.6), channel_id=1, replica_groups=mesh['groups'=2,'vid'=8,'tok'=2] {'tok'}, dimensions={2}, use_global_device_ids=true | all-gather | bytes 27648 | tf_op jit(solution)/shard_map/all_gather | solution.py:61
  159.7 0.6 copy.17
  (122 shorter events, 15.5 us)
Async XLA Ops:
  6.5 5.7 %copy-start.3 = (s32[1,128]{1,0:T(1,128)S(1)}, s32[1,128]{1,0:T(1,128)}, u32[]{:S(2)}) copy-start(s32[1,128]{1,0:T(1,128)} %param.11) | copy-start | bytes 1540
  6.5 19.3 %copy-start.2 = (bf16[12,128,128]{2,1,0:T(8,128)(2,1)S(1)}, bf16[12,128,128]{2,1,0:T(8,128)(2,1)}, u32[]{:S(2)}) copy-start(bf16[12,128,128]{2,1,0:T(8,128)(2,1)} %param.12) | copy-start | bytes 1179652
  6.5 98.1 %all-reduce.4.cloned.1.call-start = ((), (), s32[]{:S(2)}) async-start(), calls=%async_computation | async-start | bytes 3145728 | tf_op jit(solution)/shard_map/psum | solution.py:14
  104.6 26.0 %copy-start.1 = (bf16[2048,128]{1,0:T(8,128)(2,1)S(1)}, bf16[2048,128]{1,0:T(8,128)(2,1)}, u32[]{:S(2)}) copy-start(bf16[2048,128]{1,0:T(8,128)(2,1)} %get-tuple-element.229) | copy-start | bytes 1572868
  130.6 13.4 %copy-start = (bf16[2048,128]{1,0:T(8,128)(2,1)S(1)}, bf16[2048,128]{1,0:T(8,128)(2,1)}, u32[]{:S(2)}) copy-start(bf16[2048,128]{1,0:T(8,128)(2,1)} %get-tuple-element.211) | copy-start | bytes 1572868
Sparse Core Ops, SparseCore 0:
  12.3 92.2 all-reduce.3
where the time goes:
time: 168 us; the launch traced here: 167 us
  waiting for transfers between devices  76.2 us (45%)
  matrix products  31.9 us (19%)
  blocking collectives  17.9 us (11%)
  between operations  15.4 us (9%)
  other arithmetic  14.1 us (8%)
  local copies, waits for them, and re-layouts  10.4 us (6%)
    psum x1, waiting for transfers between devices, spread(): return lax.psum(kept, axis)  76.2 us
    dot_general x36, matrix products, whole_video(): lax.dot_general(query_rows, footage_key_matrix, (((1,), (1,)), ((), ())),...  28.5 us
    psum x1, blocking collectives, spread(): return lax.psum(kept, axis)  13.5 us
    reduce_sum x36, other arithmetic, whole_video(): jnp.sum(jnp.exp(raw_similarity - row_peak[:, None]), axis=1)  11.1 us
    dynamic_update_slice x36, local copies, waits for them, and re-layouts, per_device(): lax.map(whole_video, bank_whole)  7.37 us
  transfers between devices with their start and end apart: 1, of which 1 were waited for; matrix products, arithmetic and copies ran while one was open for 0% of the time, Pallas kernels for 0%

commit v1 on v0

v1 whole, which is shorter than its diff:
```python
import jax
import jax.numpy as jnp
from jax import lax
from jax.experimental import pallas as pl
from jax.experimental.pallas import tpu as pltpu
from jax.sharding import PartitionSpec as P

SHARPNESS = 5.0
LOG2E = 1.4426950408889634
LN2 = 0.6931471805599453
COUNT_ROWS = 8
PAIR = 2


def score_kernel(slots, caps, q_ref, own_ref, tok_ref, pair_ref, both_ref, out_ref, top_ref, sum_ref):
    videos = own_ref.shape[0]
    rows = caps * slots
    query = q_ref[0, :rows, :]
    scale = jnp.float32(SHARPNESS * LOG2E)

    def one(v, at, a_ref, b_ref):
        parts = []
        for ref in (a_ref, b_ref):
            raw = lax.dot_general(
                ref[v], query, (((1,), (1,)), ((), ())), preferred_element_type=jnp.float32
            )
            parts.append((raw * scale).reshape(raw.shape[0] // 8, 8, rows))
        top = jnp.maximum(jnp.max(parts[0], axis=0), jnp.max(parts[1], axis=0))
        total = jnp.sum(jnp.exp2(parts[0] - top[None]), axis=0)
        total = total + jnp.sum(jnp.exp2(parts[1] - top[None]), axis=0)
        top_ref[at] = top
        sum_ref[at] = total

    def step(v, carry):
        one(v, v, own_ref, tok_ref)
        one(v, v + videos, pair_ref, both_ref)
        return carry

    lax.fori_loop(0, videos, step, 0)

    tops = top_ref[...]
    peak = jnp.max(tops, axis=1)
    total = jnp.sum(sum_ref[...] * jnp.exp2(tops - peak[:, None, :]), axis=1)
    soft = (peak + jnp.log2(total)) * jnp.float32(LN2 / SHARPNESS)

    counts = q_ref[0, rows : rows + 8, :].astype(jnp.float32)[0:1, :]
    row = lax.broadcasted_iota(jnp.int32, (rows, 128), 0)
    cap = lax.broadcasted_iota(jnp.int32, (rows, 128), 1)
    first = cap * slots
    last = first + counts.astype(jnp.int32)
    member = ((row >= first) & (row < last) & (cap < caps)).astype(jnp.float32)
    picked = lax.dot_general(
        soft, member, (((1,), (0,)), ((), ())),
        precision=lax.Precision.HIGHEST, preferred_element_type=jnp.float32,
    )
    out_ref[0] = picked / jnp.maximum(counts, 1.0)


def per_device(captions, caption_lengths, video_bank, owner_order):
    n_vid, n_tok = lax.axis_size("vid"), lax.axis_size("tok")
    capb, slots, width = captions.shape[1:]
    videos = video_bank.shape[0]
    rounds = owner_order.shape[0]
    line = n_vid // PAIR
    caps = capb // (n_vid * n_tok)
    rows = caps * slots
    tok = lax.axis_index("tok")
    side = lax.axis_index("vid") % PAIR

    swap_tok = [(0, 1), (1, 0)]
    swap_pair = [(i, i ^ 1) for i in range(n_vid)]
    tok_bank = lax.ppermute(video_bank, "tok", swap_tok)
    pair_bank = lax.ppermute(video_bank, "vid", swap_pair)
    both_bank = lax.ppermute(pair_bank, "tok", swap_tok)

    split = captions.reshape(PAIR, n_tok, line, rows, width)
    mine = lax.dynamic_index_in_dim(split, tok, 1, keepdims=False)
    counts = caption_lengths.reshape(PAIR, n_tok, line, 1, caps)
    counts = lax.dynamic_index_in_dim(counts, tok, 1, keepdims=False).astype(captions.dtype)
    counts = jnp.pad(counts, ((0, 0), (0, 0), (0, COUNT_ROWS - 1), (0, width - caps)))
    pieces = jnp.concatenate([mine, counts], axis=2)
    pieces = pieces.transpose(1, 0, 2, 3).reshape(n_vid, rows + COUNT_ROWS, width)
    shares = lax.all_to_all(pieces, "vid", 0, 0, tiled=True)
    wanted = jnp.stack(
        [lax.dynamic_index_in_dim(shares, owner_order[r], 0, keepdims=False) for r in range(rounds)]
    )
    lines = [[k * PAIR + s for k in range(line)] for s in range(PAIR)]
    query = lax.all_gather(wanted, "vid", axis=0, tiled=True, axis_index_groups=lines)

    whole = lambda shape: pl.BlockSpec(shape, lambda i: (0,) * len(shape))
    tiles = line * rounds
    scores = pl.pallas_call(
        lambda *refs: score_kernel(slots, caps, *refs),
        grid=(tiles,),
        in_specs=[pl.BlockSpec((1, rows + COUNT_ROWS, width), lambda i: (i, 0, 0))]
        + [whole(video_bank.shape)] * 4,
        out_specs=pl.BlockSpec((1, 2 * videos, 128), lambda i: (i, 0, 0)),
        out_shape=jax.ShapeDtypeStruct((tiles, 2 * videos, 128), jnp.float32),
        scratch_shapes=[pltpu.VMEM((2 * videos, 8, rows), jnp.float32)] * 2,
        name="soft_scores",
    )(query, video_bank, tok_bank, pair_bank, both_bank)

    scores = scores[:, :, :caps].reshape(line, rounds, PAIR, videos, caps)
    scores = scores.transpose(2, 3, 1, 0, 4).reshape(PAIR, videos, rounds, line * caps)
    theirs = lax.ppermute(scores[1], "vid", swap_pair)
    halves = jnp.stack([scores[0], theirs])
    halves = jnp.where(side == 0, halves, halves[::-1])
    other = lax.ppermute(halves, "tok", swap_tok)
    quarters = jnp.stack([jnp.where(tok == 0, halves, other), jnp.where(tok == 0, other, halves)])
    return quarters.transpose(2, 3, 1, 0, 4).reshape(videos, rounds * capb)


def solution(mesh):
    return jax.shard_map(
        per_device,
        mesh=mesh,
        in_specs=(
            P(("groups", "vid"), None, None, None),
            P(("groups", "vid"), None),
            P(("groups", "vid"), "tok", None),
            P("groups"),
        ),
        out_specs=P(("groups", "vid"), None),
        check_vma=False,
    )
```

time: 168 us -> 108 us (0.64)
  waiting for transfers between devices: 76.2 us -> 13.3 us
  Pallas kernels: 0 us -> 50.8 us
  matrix products: 31.9 us -> 0 us
  other arithmetic: 14.1 us -> 2.39 us
  between operations: 15.4 us -> 5.64 us
  starting transfers between devices: 0.01 us -> 9.75 us
  local copies, waits for them, and re-layouts: 10.4 us -> 5.08 us
  blocking collectives: 17.9 us -> 20.2 us
    psum x1 -> x0, waiting for transfers between devices: 76.2 us -> none  [spread(): return lax.psum(kept, axis)]
    pallas_call x0 -> x1, Pallas kernels: none -> 50.8 us  [per_device(): pl.pallas_call(lambda *refs: score_kernel(slots, caps, *refs), grid=(tile...]
    dot_general x39 -> x0, matrix products: 31.9 us -> none  [the longest x36 28.5 us: whole_video(): lax.dot_general(query_rows, footage_key_matrix, (((1,), (1,)), ((), ())),...]
    all_gather x2 -> x1, blocking collectives: 4.36 us -> 20.2 us  [per_device(): lax.all_gather(wanted, 'vid', axis=0, tiled=True, axis_index_groups=lines)]
    psum x1 -> x0, blocking collectives: 13.5 us -> none  [spread(): return lax.psum(kept, axis)]
    ppermute x0 -> x5, waiting for transfers between devices: none -> 13.3 us  [the longest x1 8.41 us: per_device(): pair_bank = lax.ppermute(video_bank, 'vid', swap_pair)]
    reduce_sum x36 -> x0, other arithmetic: 11.1 us -> none  [whole_video(): jnp.sum(jnp.exp(raw_similarity - row_peak[:, None]), axis=1)]
    dynamic_update_slice x36 -> x0, local copies, waits for them, and re-layouts: 7.37 us -> none  [per_device(): lax.map(whole_video, bank_whole)]
  transfers between devices with their start and end apart: 1 -> 6, of which waited for: 1 -> 3; matrix products, arithmetic and copies ran while one was open for 0% -> 1% of each run, Pallas kernels for 0% -> 0%
where the time goes in v1:
time: 108 us; the launch traced here: 107 us
  Pallas kernels  50.8 us (47%)
  blocking collectives  20.2 us (19%)
  waiting for transfers between devices  13.3 us (12%)
  starting transfers between devices  9.75 us (9%)
  between operations  5.64 us (5%)
  local copies, waits for them, and re-layouts  5.08 us (5%)
  other arithmetic  2.39 us (2%)
    pallas_call x1, Pallas kernels, per_device(): pl.pallas_call(lambda *refs: score_kernel(slots, caps, *refs), grid=(tile...  50.8 us
    all_gather x1, blocking collectives, per_device(): lax.all_gather(wanted, 'vid', axis=0, tiled=True, axis_index_groups=lines)  20.2 us
    ppermute x1, waiting for transfers between devices, per_device(): pair_bank = lax.ppermute(video_bank, 'vid', swap_pair)  8.41 us
    all_to_all x1, starting transfers between devices, per_device(): shares = lax.all_to_all(pieces, 'vid', 0, 0, tiled=True)  7.31 us
    ppermute x1, waiting for transfers between devices, per_device(): theirs = lax.ppermute(scores[1], 'vid', swap_pair)  3.71 us
  transfers between devices with their start and end apart: 6, of which 3 were waited for; matrix products, arithmetic and copies ran while one was open for 1% of the time, Pallas kernels for 0%

profile of v1, /device:TPU:0, one launch (start us, length us, event | category | flops | bytes accessed | tf_op | source)
XLA Modules:
  0.0 107.2 jit_solution(7061939409610032232)
XLA Ops:
  0.0 0.0 copy-start
  0.0 0.5 broadcast.10
  0.5 1.3 %reduce.3 = s32[128]{0:T(128)S(1)} reduce(s32[1,128]{1,0:T(1,128)} %param.5, s32[]{:T(128)} %broadcast.10), dimensions={0}, to_apply=%param.5.reduce_sub_computation.3 | reduce | bytes 1028 | tf_op args[1]
  1.8 0.1 reshape.33
  1.9 0.0 copy-done
  2.0 0.0 copy-start.1
  2.0 0.0 copy-start.5
  2.0 0.8 fusion.1
  2.9 7.3 %all-to-all-start = ((bf16[8,264,128]{2,1,0:T(8,128)(2,1)}), bf16[8,264,128]{2,1,0:T(8,128)(2,1)S(1)}, u32[]{:S(2)}, u32[]{:S(2)}) async-start(bf16[8,264,128]{2,1,0:T(8,128)(2,1)} %bitcast.4), calls=%async_computation | async-start | bytes 1081344 | tf_op jit(solution)/shard_map/all_to_all | solution.py:83
  10.2 0.0 copy-done.1
  10.2 2.0 %collective-permute-start.1 = (bf16[12,128,128]{2,1,0:T(8,128)(2,1)S(1)}, bf16[12,128,128]{2,1,0:T(8,128)(2,1)S(1)}, u32[]{:S(2)}, u32[]{:S(2)}) collective-permute-start(bf16[12,128,128]{2,1,0:T(8,128)(2,1)S(1)} %copy-done.1), channel_id=1, source_target_pairs={{0,2},{2,0},{4,6},{6,4},{8,10},{10,8},{12,14},{14,12},{1,3},{3,1},... | collective-permute-start | bytes 1179656 | tf_op jit(solution)/shard_map/ppermute | solution.py:73
  12.2 0.0 collective-permute-start
  12.2 0.0 copy-done.5
  12.2 0.6 fusion.4
  18.3 8.4 %collective-permute-done.1.refs_3_ = bf16[12,128,128]{2,1,0:T(8,128)(2,1)S(1)} collective-permute-done((bf16[12,128,128]{2,1,0:T(8,128)(2,1)S(1)}, bf16[12,128,128]{2,1,0:T(8,128)(2,1)S(1)}, u32[]{:S(2)}, u32[]{:S(2)}) %collective-permute-start.1) | collective-permute-done | bytes 393248 | tf_op jit(solution)/shard_map/ppermute | solution.py:73
  26.8 0.0 copy-start.2
  26.8 0.0 collective-permute-start.2
  26.8 0.0 all-to-all-done
  26.8 20.2 %all_gather.3.refs_0_ = bf16[12,264,128]{2,1,0:T(8,128)(2,1)} all-gather(bf16[3,264,128]{2,1,0:T(8,128)(2,1)S(1)} %pad_maximum_fusion), channel_id=1, replica_groups={{0,4,8,12},{2,6,10,14},{1,5,9,13},{3,7,11,15},{16,20,24,28},{18,22,26,3..., dimensions={0}, use_global_device_ids=true | all-gather | bytes 1013760 | tf_op jit(solution)/shard_map/all_gather | solution.py:88
  47.0 0.0 collective-permute-done.refs_2_
  47.0 0.0 copy-start.3
  47.0 0.0 collective-permute-done.2.refs_4_
  47.0 0.0 copy-done.2
  47.0 0.7 copy-done.3
  47.8 0.0 copy-start.4
  47.8 0.7 copy-done.4
  48.5 50.8 %soft_scores.1 = f32[12,24,128]{2,1,0:T(8,128)} custom-call(bf16[12,264,128]{2,1,0:T(8,128)(2,1)} %all_gather.3.refs_0_, bf16[12,128,128]{2,1,0:T(8,128)(2,1)} %refs_1_.1, bf16[12,128,128]{2,1,0:T(8,128)(2,1)} %copy-done.3, bf16[12,128,128]{2,1,0:T(8,128)(2,1)} %copy-done.2, bf16[12,128,128]{2,1,0:T(8,128)(2,1)} %copy-done.4), custom_call_target="tpu_custom_call" | custom-call | tf_op jit(solution)/shard_map/soft_scores/pallas_call | solution.py:92
  99.3 1.0 copy.21
  100.3 0.1 reshape.35
  100.4 0.1 fusion.3
  100.5 0.3 collective-permute-start.3
  100.9 0.1 copy.24
  101.0 3.7 %collective-permute-done.3 = f32[12,3,32]{0,2,1:T(8,128)S(1)} collective-permute-done((f32[12,3,32]{0,2,1:T(8,128)S(1)}, f32[12,3,32]{0,2,1:T(8,128)S(1)}, u32[]{:S(2)}, u32[]{:S(2)}) %collective-permute-start.3) | collective-permute-done | bytes 4640 | tf_op jit(solution)/shard_map/ppermute | solution.py:105
  104.7 0.1 copy.25
  104.8 0.1 rev.3
  104.9 0.1 broadcast_select_fusion
  105.0 0.1 collective-permute-start.4
  105.1 1.2 %collective-permute-done.4 = f32[2,12,3,32]{3,0,2,1:T(2,128)S(1)} collective-permute-done((f32[2,12,3,32]{3,0,2,1:T(2,128)S(1)}, f32[2,12,3,32]{3,0,2,1:T(2,128)S(1)}, u32[]{:S(2)}, u32[]{:S(2)}) %collective-permute-start.4) | collective-permute-done | bytes 9248 | tf_op jit(solution)/shard_map/ppermute | solution.py:108
  106.3 0.1 select_bitcast_fusion.1
  106.4 0.7 reshape.36
  (10 shorter events, 0.2 us)
Async XLA Ops:
  0.0 1.9 %copy-start = (bf16[1,128,32,128]{3,2,1,0:T(8,128)(2,1)S(1)}, bf16[1,128,32,128]{3,2,1,0:T(8,128)(2,1)}, u32[]{:S(2)}) copy-start(bf16[1,128,32,128]{3,2,1,0:T(8,128)(2,1)} %param.4) | copy-start | bytes 3145732
  2.0 8.2 %copy-start.1 = (bf16[12,128,128]{2,1,0:T(8,128)(2,1)S(1)}, bf16[12,128,128]{2,1,0:T(8,128)(2,1)}, u32[]{:S(2)}) copy-start(bf16[12,128,128]{2,1,0:T(8,128)(2,1)} %refs_1_.1) | copy-start | bytes 1179652
  2.0 10.2 %copy-start.5 = (s32[3]{0:T(128)S(1)}, s32[3]{0:T(128)}, u32[]{:S(2)}) copy-start(s32[3]{0:T(128)} %param.7) | copy-start | bytes 40
  2.9 23.9 %all-to-all-start = ((bf16[8,264,128]{2,1,0:T(8,128)(2,1)}), bf16[8,264,128]{2,1,0:T(8,128)(2,1)S(1)}, u32[]{:S(2)}, u32[]{:S(2)}) async-start(bf16[8,264,128]{2,1,0:T(8,128)(2,1)} %bitcast.4), calls=%async_computation | async-start | bytes 1081344 | tf_op jit(solution)/shard_map/all_to_all | solution.py:83
  10.2 16.6 %collective-permute-start.1 = (bf16[12,128,128]{2,1,0:T(8,128)(2,1)S(1)}, bf16[12,128,128]{2,1,0:T(8,128)(2,1)S(1)}, u32[]{:S(2)}, u32[]{:S(2)}) collective-permute-start(bf16[12,128,128]{2,1,0:T(8,128)(2,1)S(1)} %copy-done.1), channel_id=1, source_target_pairs={{0,2},{2,0},{4,6},{6,4},{8,10},{10,8},{12,14},{14,12},{1,3},{3,1},... | collective-permute-start | bytes 1179656 | tf_op jit(solution)/shard_map/ppermute | solution.py:73
  12.2 34.8 %collective-permute-start = (bf16[12,128,128]{2,1,0:T(8,128)(2,1)S(1)}, bf16[12,128,128]{2,1,0:T(8,128)(2,1)S(1)}, u32[]{:S(2)}, u32[]{:S(2)}) collective-permute-start(bf16[12,128,128]{2,1,0:T(8,128)(2,1)S(1)} %copy-done.1), channel_id=1, source_target_pairs={{0,1},{1,0},{2,3},{3,2},{4,5},{5,4},{6,7},{7,6},{8,9},{9,8},{10,11... | collective-permute-start | bytes 1179656 | tf_op jit(solution)/shard_map/ppermute | solution.py:72
  26.8 20.3 %copy-start.2 = (bf16[12,128,128]{2,1,0:T(8,128)(2,1)}, bf16[12,128,128]{2,1,0:T(8,128)(2,1)S(1)}, u32[]{:S(2)}) copy-start(bf16[12,128,128]{2,1,0:T(8,128)(2,1)S(1)} %collective-permute-done.1.refs_3_) | copy-start | bytes 1179652
  26.8 20.3 %collective-permute-start.2 = (bf16[12,128,128]{2,1,0:T(8,128)(2,1)S(1)}, bf16[12,128,128]{2,1,0:T(8,128)(2,1)S(1)}, u32[]{:S(2)}, u32[]{:S(2)}) collective-permute-start(bf16[12,128,128]{2,1,0:T(8,128)(2,1)S(1)} %collective-permute-done.1.refs_3_), channel_id=1, source_target_pairs={{0,1},{1,0},{2,3},{3,2},{4,5},{5,4},{6,7},{7,6},{8,9},{9,8},{10,11... | collective-permute-start | bytes 1179656 | tf_op jit(solution)/shard_map/ppermute | solution.py:74
  47.0 0.8 copy-start.3
  47.8 0.8 copy-start.4
  100.5 4.2 %collective-permute-start.3 = (f32[12,3,32]{0,2,1:T(8,128)S(1)}, f32[12,3,32]{0,2,1:T(8,128)S(1)}, u32[]{:S(2)}, u32[]{:S(2)}) collective-permute-start(f32[12,3,32]{0,2,1:T(8,128)S(1)} %bitcast.32), channel_id=1, source_target_pairs={{0,2},{2,0},{4,6},{6,4},{8,10},{10,8},{12,14},{14,12},{1,3},{3,1},... | collective-permute-start | bytes 13832 | tf_op jit(solution)/shard_map/ppermute | solution.py:105
  105.0 1.3 %collective-permute-start.4 = (f32[2,12,3,32]{3,0,2,1:T(2,128)S(1)}, f32[2,12,3,32]{3,0,2,1:T(2,128)S(1)}, u32[]{:S(2)}, u32[]{:S(2)}) collective-permute-start(f32[2,12,3,32]{3,0,2,1:T(2,128)S(1)} %broadcast_select_fusion), channel_id=1, source_target_pairs={{0,1},{1,0},{2,3},{3,2},{4,5},{5,4},{6,7},{7,6},{8,9},{9,8},{10,11... | collective-permute-start | bytes 27656 | tf_op jit(solution)/shard_map/ppermute | solution.py:108

commit v2 on v0

v2 whole, which is shorter than its diff:
```python
import jax
import jax.numpy as jnp
from jax import lax
from jax.experimental import pallas as pl
from jax.experimental.pallas import tpu as pltpu
from jax.sharding import PartitionSpec as P

SHARPNESS = 5.0
LOG2E = 1.4426950408889634
LN2 = 0.6931471805599453
COUNT_ROWS = 8
PAIR = 2
TILE = 256
LANES = 128
JOBS = 2
VMEM_BYTES = 24 << 20
F32 = jnp.float32
BF16 = jnp.bfloat16


def dot(a, b, dims):
    return lax.dot_general(a, b, (dims, ((), ())), preferred_element_type=F32)


def score_kernel(slots, caps, meta_ref, lanes_ref, q_hbm, own_ref, tok_ref, pair_ref, both_ref,
                 out_ref, q_ref, bank_ref, rows_ref, soft_ref, a_ref, b_ref, sems):
    line, rounds = q_ref.shape[:2]
    quarters = LANES // (line * caps)
    videos, half = own_ref.shape[:2]
    tokens = 2 * half
    fetch_q = pltpu.make_async_copy(q_hbm, q_ref, sems.at[0])
    fetch_q.start()
    banks = []
    for k, src in enumerate((own_ref, tok_ref, pair_ref, both_ref)):
        dst = bank_ref.at[pl.ds(k // 2 * videos, videos), pl.ds(k % 2 * half, half), :]
        banks.append(pltpu.make_async_copy(src, dst, sems.at[1 + k]))
        banks[-1].start()
    fetch_q.wait()
    total_rows, quarter = meta_ref[2 * rounds, 0], meta_ref[2 * rounds, 1]

    def pack(i, carry):
        r, g = i // line, i % line
        piece = q_ref[g, r].astype(F32)
        for c in range(caps):
            start = meta_ref[r, (g * quarters + quarter) * caps + c]
            rows_ref[pl.ds(start, slots), :] = piece[c * slots : (c + 1) * slots]
        return carry

    lax.fori_loop(0, rounds * line, pack, 0)
    for copy in banks:
        copy.wait()
    out_ref[...] = jnp.zeros_like(out_ref)
    scale = F32(SHARPNESS * LOG2E)
    per = 2 * videos // JOBS
    jobs = [k * per for k in range(JOBS)]
    bufs = (a_ref, b_ref)

    def products(dst, first, w):
        bank = bank_ref[first : first + per].reshape(per * tokens, bank_ref.shape[2])
        dst[...] = dot(jnp.concatenate([bank, bank], axis=1), w, ((1,), (1,)))

    def unit(src, v, col):
        x = src[v * tokens : (v + 1) * tokens, col : col + LANES].reshape(tokens // 8, 8, LANES)
        top = jnp.max(x, axis=0)
        total = jnp.sum(jnp.exp2(x - top[None]), axis=0)
        peak = jnp.max(top, axis=0, keepdims=True)
        return peak, jnp.sum(total * jnp.exp2(top - peak), axis=0, keepdims=True)

    def weights(i):
        q = rows_ref[pl.ds(pl.multiple_of(i * TILE, TILE), TILE), :] * scale
        high = q.astype(BF16)
        return jnp.concatenate([high, (q - high.astype(F32)).astype(BF16)], axis=1)

    def collect(i):
        soft = (soft_ref[0] + jnp.log2(soft_ref[1])) * F32(LN2 / SHARPNESS)
        col = i * TILE + lax.broadcasted_iota(jnp.int32, soft.shape, 1)
        soft = jnp.where((col >= 0) & (col < total_rows), soft, 0.0)
        parts = []
        for _ in range(3):
            parts.append(soft.astype(BF16))
            soft = soft - parts[-1].astype(F32)
        parts = jnp.concatenate(parts, axis=0)
        row = i * TILE + lax.broadcasted_iota(jnp.int32, (TILE, LANES), 0)
        n = 2 * videos
        for r in range(rounds):
            first, count = lanes_ref[r : r + 1, :], lanes_ref[rounds + r : rounds + r + 1, :]
            member = jnp.where((row >= first) & (row < first + count), F32(1), F32(0))
            got = dot(parts, member.astype(BF16), ((1,), (0,)))
            out_ref[:, r * LANES : (r + 1) * LANES] += got[:n] + got[n : 2 * n] + got[2 * n :]

    def tile(i, carry):
        w = weights(i)
        collect(i - 1)
        for j, first in enumerate(jobs):
            after = (jobs[j + 1], w) if j + 1 < len(jobs) else (jobs[0], weights(i + 1))
            products(bufs[(j + 1) % 2], *after)
            for v in range(per):
                for col in range(0, TILE, LANES):
                    peak, total = unit(bufs[j % 2], v, col)
                    at = first + v
                    soft_ref[0, at : at + 1, col : col + LANES] = peak
                    soft_ref[1, at : at + 1, col : col + LANES] = total
        return carry

    products(bufs[0], jobs[0], weights(0))
    tiles = (total_rows + TILE - 1) // TILE
    lax.fori_loop(0, tiles, tile, 0)
    collect(tiles - 1)
    for r in range(rounds):
        count = jnp.maximum(lanes_ref[rounds + r : rounds + r + 1, :], 1).astype(F32)
        out_ref[:, r * LANES : (r + 1) * LANES] = out_ref[:, r * LANES : (r + 1) * LANES] / count


def pair_scores(slots, caps, meta, query, banks):
    line, rounds, rows, width = query.shape
    videos, half = banks[0].shape[:2]
    n_rows = -(-(rounds * line * rows) // TILE) * TILE + TILE + slots
    vmem = pl.BlockSpec(memory_space=pltpu.VMEM)
    anywhere = pl.BlockSpec(memory_space=pl.ANY)
    return pl.pallas_call(
        lambda *refs: score_kernel(slots, caps, *refs),
        in_specs=[pl.BlockSpec(memory_space=pltpu.SMEM), vmem] + [anywhere] * 5,
        out_specs=vmem,
        out_shape=jax.ShapeDtypeStruct((2 * videos, rounds * LANES), F32),
        scratch_shapes=[
            pltpu.VMEM(query.shape, query.dtype),
            pltpu.VMEM((2 * videos, 2 * half, width), banks[0].dtype),
            pltpu.VMEM((n_rows, width), F32),
            pltpu.VMEM((2, 2 * videos, TILE), F32),
            pltpu.VMEM((2 * videos // JOBS * 2 * half, TILE), F32),
            pltpu.VMEM((2 * videos // JOBS * 2 * half, TILE), F32),
            pltpu.SemaphoreType.DMA((5,)),
        ],
        compiler_params=pltpu.CompilerParams(vmem_limit_bytes=VMEM_BYTES),
        name="soft_scores",
    )(meta, meta, query, *banks)


def per_device(captions, caption_lengths, video_bank, owner_order):
    n_vid, n_tok = lax.axis_size("vid"), lax.axis_size("tok")
    capb, slots, width = captions.shape[1:]
    rounds = owner_order.shape[0]
    videos = video_bank.shape[0]
    line = n_vid // PAIR
    caps = capb // (n_vid * n_tok)
    rows = caps * slots
    tok = lax.axis_index("tok")
    quarter = lax.axis_index("vid") % PAIR * n_tok + tok
    swap_tok = [(0, 1), (1, 0)]
    swap_pair = [(i, i ^ 1) for i in range(n_vid)]

    tok_bank = lax.ppermute(video_bank, "tok", swap_tok)
    pair_bank = lax.ppermute(video_bank, "vid", swap_pair)
    both_bank = lax.ppermute(tok_bank, "vid", swap_pair)

    mine = lax.dynamic_index_in_dim(
        captions.reshape(n_vid, n_tok, rows, width), tok, 1, keepdims=False
    )
    counts = jnp.pad(caption_lengths.astype(captions.dtype), ((0, COUNT_ROWS - 1), (0, width - capb)))
    counts = jnp.broadcast_to(counts, (n_vid, COUNT_ROWS, width))
    pieces = jnp.concatenate([mine, counts], axis=1)
    shares = lax.all_to_all(pieces, "vid", 0, 0, tiled=True)
    owners = [owner_order[r] for r in range(rounds)]
    wanted = jnp.concatenate(
        [lax.dynamic_index_in_dim(shares, o, 0, keepdims=False)[:rows] for o in owners]
    )
    lines = [[k * PAIR + s for k in range(line)] for s in range(PAIR)]
    query = lax.all_gather(wanted, "vid", axis=0, axis_index_groups=lines)
    query = query.reshape(line, rounds, rows, width)

    counts = jnp.concatenate(
        [lax.dynamic_slice(shares, (o, rows, 0), (1, 1, capb)).reshape(1, capb) for o in owners]
    ).astype(jnp.int32)
    lane = jnp.arange(capb, dtype=jnp.int32)
    counts = jnp.where(lane // caps % (PAIR * n_tok) == quarter, counts, 0)
    flat = counts.reshape(rounds * capb)
    place = jnp.arange(rounds * capb, dtype=jnp.int32)
    starts = jnp.sum(jnp.where(place[None, :] < place[:, None], flat[None, :], 0), axis=1)
    tail = jnp.where(lane == 0, jnp.sum(flat), jnp.where(lane == 1, quarter, 0))
    meta = jnp.concatenate([starts.reshape(rounds, capb), counts, tail[None]])
    meta = jnp.pad(meta, ((0, -meta.shape[0] % 8), (0, 0)))

    scores = pair_scores(slots, caps, meta, query, (video_bank, tok_bank, pair_bank, both_bank))
    scores = scores[:videos] + lax.ppermute(scores[videos:], "vid", swap_pair)
    return scores + lax.ppermute(scores, "tok", swap_tok)


def solution(mesh):
    return jax.shard_map(
        per_device,
        mesh=mesh,
        in_specs=(
            P(("groups", "vid"), None, None, None),
            P(("groups", "vid"), None),
            P(("groups", "vid"), "tok", None),
            P("groups"),
        ),
        out_specs=P(("groups", "vid"), None),
        check_vma=False,
    )
```

time: 168 us -> 61.6 us (0.37)
  waiting for transfers between devices: 76.2 us -> 9.79 us
  matrix products: 31.9 us -> 0 us
  Pallas kernels: 0 us -> 11.9 us
  starting transfers between devices: 0.01 us -> 11.2 us
  other arithmetic: 14.1 us -> 3.68 us
  between operations: 15.4 us -> 5.71 us
  local copies, waits for them, and re-layouts: 10.4 us -> 1.21 us
    psum x1 -> x0, waiting for transfers between devices: 76.2 us -> none  [spread(): return lax.psum(kept, axis)]
    dot_general x39 -> x0, matrix products: 31.9 us -> none  [the longest x36 28.5 us: whole_video(): lax.dot_general(query_rows, footage_key_matrix, (((1,), (1,)), ((), ())),...]
    psum x1 -> x0, blocking collectives: 13.5 us -> none  [spread(): return lax.psum(kept, axis)]
    all_gather x2 -> x1, blocking collectives: 4.36 us -> 17.8 us  [per_device(): query = lax.all_gather(wanted, 'vid', axis=0, axis_index_groups=lines)]
    pallas_call x0 -> x1, Pallas kernels: none -> 11.9 us  [pair_scores(): pl.pallas_call(lambda *refs: score_kernel(slots, caps, *refs), in_specs=[...]
    reduce_sum x36 -> x1, other arithmetic: 11.1 us -> 0.14 us  [per_device(): jnp.sum(jnp.where(place[None, :] < place[:, None], flat[None, :], 0), axi...]
    dynamic_update_slice x36 -> x0, local copies, waits for them, and re-layouts: 7.37 us -> none  [per_device(): lax.map(whole_video, bank_whole)]
    all_to_all x0 -> x1, starting transfers between devices: none -> 7.31 us  [per_device(): shares = lax.all_to_all(pieces, 'vid', 0, 0, tiled=True)]
  transfers between devices with their start and end apart: 1 -> 6, of which waited for: 1 -> 3; matrix products, arithmetic and copies ran while one was open for 0% -> 3% of each run, Pallas kernels for 0% -> 0%
where the time goes in v2:
time: 61.6 us; the launch traced here: 61.3 us
  blocking collectives  17.8 us (29%)
  Pallas kernels  11.9 us (19%)
  starting transfers between devices  11.2 us (18%)
  waiting for transfers between devices  9.79 us (16%)
  between operations  5.71 us (9%)
  other arithmetic  3.68 us (6%)
  local copies, waits for them, and re-layouts  1.21 us (2%)
    all_gather x1, blocking collectives, per_device(): query = lax.all_gather(wanted, 'vid', axis=0, axis_index_groups=lines)  17.8 us
    pallas_call x1, Pallas kernels, pair_scores(): pl.pallas_call(lambda *refs: score_kernel(slots, caps, *refs), in_specs=[...  11.9 us
    all_to_all x1, starting transfers between devices, per_device(): shares = lax.all_to_all(pieces, 'vid', 0, 0, tiled=True)  7.31 us
    all_to_all x1, waiting for transfers between devices, per_device(): shares = lax.all_to_all(pieces, 'vid', 0, 0, tiled=True)  6.37 us
    ppermute x1, waiting for transfers between devices, per_device(): scores = scores[:videos] + lax.ppermute(scores[videos:], 'vid', swap_pair)  2.22 us
    ppermute x1, starting transfers between devices, per_device(): pair_bank = lax.ppermute(video_bank, 'vid', swap_pair)  2.01 us
    ppermute x1, starting transfers between devices, per_device(): scores = scores[:videos] + lax.ppermute(scores[videos:], 'vid', swap_pair)  1.67 us
  transfers between devices with their start and end apart: 6, of which 3 were waited for; matrix products, arithmetic and copies ran while one was open for 3% of the time, Pallas kernels for 0%

profile of v2, /device:TPU:0, one launch (start us, length us, event | category | flops | bytes accessed | tf_op | source)
XLA Modules:
  0.0 61.3 jit_solution(3766263484909680233)
XLA Ops:
  0.0 0.0 copy-start
  0.0 0.7 %convert_element_type.15 = bf16[1,128]{1,0:T(2,128)(2,1)S(1)} convert(s32[1,128]{1,0:T(1,128)} %param.5) | non-fusion elementwise | flops 128 | bytes 768 | tf_op jit(solution)/shard_map/convert_element_type | solution.py:159
  0.8 0.5 copy-done
  1.3 0.0 copy-start.1
  1.3 0.0 copy-start.2
  1.3 0.8 %pad_maximum_fusion = bf16[8,264,128]{2,1,0:T(8,128)(2,1)} fusion(bf16[8,8,128]{2,1,0:T(8,128)(2,1)S(1)} %broadcast_in_dim.35, bf16[8,256,128]{2,1,0:T(8,128)(2,1)S(1)} %dynamic-slice_bitcast_fusion), kind=kLoop, calls=%fused_computation.2 | loop fusion | flops 1081344 | bytes 1081344 | tf_op jit(solution)/shard_map/concatenate | solution.py:161
  2.2 7.3 %all-to-all-start = ((bf16[8,264,128]{2,1,0:T(8,128)(2,1)}), bf16[8,264,128]{2,1,0:T(8,128)(2,1)S(1)}, u32[]{:S(2)}, u32[]{:S(2)}) async-start(bf16[8,264,128]{2,1,0:T(8,128)(2,1)} %pad_maximum_fusion), calls=%async_computation | async-start | bytes 1081344 | tf_op jit(solution)/shard_map/all_to_all | solution.py:162
  9.5 0.0 copy-done.1
  9.5 0.1 collective-permute-start
  9.6 2.0 %collective-permute-start.1 = (bf16[12,128,128]{2,1,0:T(8,128)(2,1)S(1)}, bf16[12,128,128]{2,1,0:T(8,128)(2,1)S(1)}, u32[]{:S(2)}, u32[]{:S(2)}) collective-permute-start(bf16[12,128,128]{2,1,0:T(8,128)(2,1)S(1)} %copy-done.1), channel_id=1, source_target_pairs={{0,2},{2,0},{4,6},{6,4},{8,10},{10,8},{12,14},{14,12},{1,3},{3,1},... | collective-permute-start | bytes 1179656 | tf_op jit(solution)/shard_map/ppermute | solution.py:153
  11.6 0.0 copy-done.2
  11.6 0.6 fusion.7
  17.8 0.0 collective-permute-done.refs_4_
  17.8 0.1 collective-permute-start.2
  17.9 6.4 %all-to-all-done = bf16[8,264,128]{2,1,0:T(8,128)(2,1)S(1)} async-done(((bf16[8,264,128]{2,1,0:T(8,128)(2,1)}), bf16[8,264,128]{2,1,0:T(8,128)(2,1)S(1)}, u32[]{:S(2)}, u32[]{:S(2)}) %all-to-all-start) | async-done | bytes 540704 | tf_op jit(solution)/shard_map/all_to_all | solution.py:162
  24.3 0.6 %fusion.6 = (s32[384]{0:T(512)S(1)}, s32[]{:T(128)}, s32[3,128]{1,0:T(4,128)S(1)}) fusion(bf16[1,128]{1,0:T(2,128)(2,1)S(1)} %get-tuple-element.9, bf16[1,128]{1,0:T(2,128)(2,1)S(1)} %get-tuple-element.10, bf16[1,128]{1,0:T(2,128)(2,1)S(1)} %get-tuple-element.8, pred[128]{0:T(512)(128)(4,1)S(1)} %fusion.3), kind=kLoop, calls=%fused_computation.29 | loop fusion | flops 3071 | bytes 3972 | tf_op jit(solution)/shard_map/jit(_where)/select_n | solution.py:175
  25.0 0.1 select_reduce_fusion
  25.1 0.7 %compare_select_fusion.3 = s32[1,128]{1,0:T(1,128)S(1)} fusion(s32[]{:T(128)S(6)} %add.43, s32[]{:T(128)} %get-tuple-element.12), kind=kLoop, calls=%fused_computation.14 | loop fusion | flops 512 | bytes 520 | tf_op jit(solution)/shard_map/jit(_where)/select_n | solution.py:179
  25.9 17.8 %all-gather = bf16[3072,128]{1,0:T(8,128)(2,1)S(1)} all-gather(bf16[768,128]{1,0:T(8,128)(2,1)S(1)} %pad_maximum_fusion.1), channel_id=2, replica_groups={{0,4,8,12},{2,6,10,14},{1,5,9,13},{3,7,11,15},{16,20,24,28},{18,22,26,3..., dimensions={0}, use_global_device_ids=true | all-gather | bytes 983040 | tf_op jit(solution)/shard_map/all_gather | solution.py:168
  43.6 0.0 collective-permute-done.1.refs_5_
  43.6 0.0 collective-permute-done.2.refs_6_
  43.6 11.9 %soft_scores.1 = f32[24,384]{1,0:T(8,128)S(1)} custom-call(s32[8,128]{1,0:T(8,128)S(1)} %pad.9.refs_0_.refs_1_, s32[8,128]{1,0:T(8,128)S(1)} %pad.9.refs_0_.refs_1_, bf16[4,3,256,128]{3,2,1,0:T(8,128)(2,1)S(1)} %bitcast.23, bf16[12,128,128]{2,1,0:T(8,128)(2,1)S(1)} %copy-done.1, bf16[12,128,128]{2,1,0:T(8,128)(2,1)S(1)} %collective-permute-done.refs_4_, ...), custom_call_target="tpu_custom_call" | custom-call | tf_op jit(solution)/shard_map/soft_scores/pallas_call | solution.py:120
  55.5 1.7 %collective-permute-start.3 = (f32[12,384]{1,0:T(8,128)S(1)}, f32[12,384]{1,0:T(8,128)S(1)}, u32[]{:S(2)}, u32[]{:S(2)}) collective-permute-start(f32[12,384]{1,0:T(8,128)S(1)} %slice.45), channel_id=1, source_target_pairs={{0,2},{2,0},{4,6},{6,4},{8,10},{10,8},{12,14},{14,12},{1,3},{3,1},... | collective-permute-start | bytes 55304 | tf_op jit(solution)/shard_map/ppermute | solution.py:184
  57.2 2.2 %collective-permute-done.3 = f32[12,384]{1,0:T(8,128)S(1)} collective-permute-done((f32[12,384]{1,0:T(8,128)S(1)}, f32[12,384]{1,0:T(8,128)S(1)}, u32[]{:S(2)}, u32[]{:S(2)}) %collective-permute-start.3) | collective-permute-done | bytes 18464 | tf_op jit(solution)/shard_map/ppermute | solution.py:184
  59.4 0.0 collective-permute-start.4
  59.5 1.2 %collective-permute-done.4 = f32[12,384]{1,0:T(8,128)S(1)} collective-permute-done((f32[12,384]{1,0:T(8,128)S(1)}, f32[12,384]{1,0:T(8,128)S(1)}, u32[]{:S(2)}, u32[]{:S(2)}) %collective-permute-start.4) | collective-permute-done | bytes 18464 | tf_op jit(solution)/shard_map/ppermute | solution.py:185
  60.6 0.6 add.49
  (11 shorter events, 0.1 us)
Async XLA Ops:
  0.0 1.2 %copy-start = (bf16[1,128,32,128]{3,2,1,0:T(8,128)(2,1)S(1)}, bf16[1,128,32,128]{3,2,1,0:T(8,128)(2,1)}, u32[]{:S(2)}) copy-start(bf16[1,128,32,128]{3,2,1,0:T(8,128)(2,1)} %param.4) | copy-start | bytes 3145732
  1.3 8.2 %copy-start.1 = (bf16[12,128,128]{2,1,0:T(8,128)(2,1)S(1)}, bf16[12,128,128]{2,1,0:T(8,128)(2,1)}, u32[]{:S(2)}) copy-start(bf16[12,128,128]{2,1,0:T(8,128)(2,1)} %refs_3_.1) | copy-start | bytes 1179652
  1.3 10.3 %copy-start.2 = (s32[3]{0:T(128)S(1)}, s32[3]{0:T(128)}, u32[]{:S(2)}) copy-start(s32[3]{0:T(128)} %param.7) | copy-start | bytes 40
  2.2 22.1 %all-to-all-start = ((bf16[8,264,128]{2,1,0:T(8,128)(2,1)}), bf16[8,264,128]{2,1,0:T(8,128)(2,1)S(1)}, u32[]{:S(2)}, u32[]{:S(2)}) async-start(bf16[8,264,128]{2,1,0:T(8,128)(2,1)} %pad_maximum_fusion), calls=%async_computation | async-start | bytes 1081344 | tf_op jit(solution)/shard_map/all_to_all | solution.py:162
  9.5 8.3 %collective-permute-start = (bf16[12,128,128]{2,1,0:T(8,128)(2,1)S(1)}, bf16[12,128,128]{2,1,0:T(8,128)(2,1)S(1)}, u32[]{:S(2)}, u32[]{:S(2)}) collective-permute-start(bf16[12,128,128]{2,1,0:T(8,128)(2,1)S(1)} %copy-done.1), channel_id=1, source_target_pairs={{0,1},{1,0},{2,3},{3,2},{4,5},{5,4},{6,7},{7,6},{8,9},{9,8},{10,11... | collective-permute-start | bytes 1179656 | tf_op jit(solution)/shard_map/ppermute | solution.py:152
  9.6 34.0 %collective-permute-start.1 = (bf16[12,128,128]{2,1,0:T(8,128)(2,1)S(1)}, bf16[12,128,128]{2,1,0:T(8,128)(2,1)S(1)}, u32[]{:S(2)}, u32[]{:S(2)}) collective-permute-start(bf16[12,128,128]{2,1,0:T(8,128)(2,1)S(1)} %copy-done.1), channel_id=1, source_target_pairs={{0,2},{2,0},{4,6},{6,4},{8,10},{10,8},{12,14},{14,12},{1,3},{3,1},... | collective-permute-start | bytes 1179656 | tf_op jit(solution)/shard_map/ppermute | solution.py:153
  17.8 25.8 %collective-permute-start.2 = (bf16[12,128,128]{2,1,0:T(8,128)(2,1)S(1)}, bf16[12,128,128]{2,1,0:T(8,128)(2,1)S(1)}, u32[]{:S(2)}, u32[]{:S(2)}) collective-permute-start(bf16[12,128,128]{2,1,0:T(8,128)(2,1)S(1)} %collective-permute-done.refs_4_), channel_id=1, source_target_pairs={{0,2},{2,0},{4,6},{6,4},{8,10},{10,8},{12,14},{14,12},{1,3},{3,1},... | collective-permute-start | bytes 1179656 | tf_op jit(solution)/shard_map/ppermute | solution.py:154
  55.5 3.9 %collective-permute-start.3 = (f32[12,384]{1,0:T(8,128)S(1)}, f32[12,384]{1,0:T(8,128)S(1)}, u32[]{:S(2)}, u32[]{:S(2)}) collective-permute-start(f32[12,384]{1,0:T(8,128)S(1)} %slice.45), channel_id=1, source_target_pairs={{0,2},{2,0},{4,6},{6,4},{8,10},{10,8},{12,14},{14,12},{1,3},{3,1},... | collective-permute-start | bytes 55304 | tf_op jit(solution)/shard_map/ppermute | solution.py:184
  59.4 1.2 %collective-permute-start.4 = (f32[12,384]{1,0:T(8,128)S(1)}, f32[12,384]{1,0:T(8,128)S(1)}, u32[]{:S(2)}, u32[]{:S(2)}) collective-permute-start(f32[12,384]{1,0:T(8,128)S(1)} %slice_add_fusion), channel_id=1, source_target_pairs={{0,1},{1,0},{2,3},{3,2},{4,5},{5,4},{6,7},{7,6},{8,9},{9,8},{10,11... | collective-permute-start | bytes 55304 | tf_op jit(solution)/shard_map/ppermute | solution.py:185

commit v3 on v2

--- a/solution.py
+++ b/solution.py
@@ -23,7 +23,8 @@
 
 
 def score_kernel(slots, caps, meta_ref, lanes_ref, q_hbm, own_ref, tok_ref, pair_ref, both_ref,
-                 out_ref, q_ref, bank_ref, rows_ref, soft_ref, a_ref, b_ref, sems):
+                 near_ref, far_ref, q_ref, bank_ref, out_ref, rows_ref,
+                 soft_ref, a_ref, b_ref, sems):
     line, rounds = q_ref.shape[:2]
     quarters = LANES // (line * caps)
     videos, half = own_ref.shape[:2]
@@ -108,7 +109,9 @@
     collect(tiles - 1)
     for r in range(rounds):
         count = jnp.maximum(lanes_ref[rounds + r : rounds + r + 1, :], 1).astype(F32)
-        out_ref[:, r * LANES : (r + 1) * LANES] = out_ref[:, r * LANES : (r + 1) * LANES] / count
+        mean = out_ref[:, r * LANES : (r + 1) * LANES] / count
+        near_ref[:, r * LANES : (r + 1) * LANES] = mean[:videos]
+        far_ref[:, r * LANES : (r + 1) * LANES] = mean[videos:]
 
 
 def pair_scores(slots, caps, meta, query, banks):
@@ -120,11 +123,12 @@
     return pl.pallas_call(
         lambda *refs: score_kernel(slots, caps, *refs),
         in_specs=[pl.BlockSpec(memory_space=pltpu.SMEM), vmem] + [anywhere] * 5,
-        out_specs=vmem,
-        out_shape=jax.ShapeDtypeStruct((2 * videos, rounds * LANES), F32),
+        out_specs=[vmem] * 2,
+        out_shape=[jax.ShapeDtypeStruct((videos, rounds * LANES), F32)] * 2,
         scratch_shapes=[
             pltpu.VMEM(query.shape, query.dtype),
             pltpu.VMEM((2 * videos, 2 * half, width), banks[0].dtype),
+            pltpu.VMEM((2 * videos, rounds * LANES), F32),
             pltpu.VMEM((n_rows, width), F32),
             pltpu.VMEM((2, 2 * videos, TILE), F32),
             pltpu.VMEM((2 * videos // JOBS * 2 * half, TILE), F32),
@@ -136,53 +140,105 @@
     )(meta, meta, query, *banks)
 
 
+def prepare_kernel(tok_axis, block_ref, counts_ref, out_ref, piece_ref, count_ref, in_sems, out_sems):
+    n, rows = block_ref.shape[0], block_ref.shape[2]
+    tok = lax.axis_index(tok_axis)
+    lengths = pltpu.make_async_copy(counts_ref, count_ref, in_sems.at[n])
+    lengths.start()
+    moves = []
+    for k in range(n):
+        moves.append(
+            pltpu.make_async_copy(block_ref.at[k, tok], piece_ref.at[k, pl.ds(0, rows)], in_sems.at[k])
+        )
+        moves[-1].start()
+    lengths.wait()
+    counts = jnp.broadcast_to(count_ref[...], (COUNT_ROWS, LANES)).astype(F32).astype(BF16)
+    for k in range(n):
+        piece_ref[k, rows:, :] = counts
+    for k in range(n):
+        moves[k].wait()
+        moves[k] = pltpu.make_async_copy(piece_ref.at[k], out_ref.at[k], out_sems.at[k])
+        moves[k].start()
+    for move in moves:
+        move.wait()
+
+
+def pick_kernel(caps, quarters, vid_axis, tok_axis, order_ref, shares_ref, wanted_ref, meta_ref):
+    rounds = order_ref.shape[0]
+    rows = shares_ref.shape[1] - COUNT_ROWS
+    quarter = lax.axis_index(vid_axis) % PAIR * (quarters // PAIR) + lax.axis_index(tok_axis)
+    lane = lax.broadcasted_iota(jnp.int32, (1, LANES), 1)
+    mine = lane // caps % quarters == quarter
+    before = lax.broadcasted_iota(jnp.int32, (LANES, LANES), 0) < lax.broadcasted_iota(
+        jnp.int32, (LANES, LANES), 1
+    )
+    before = jnp.where(before, F32(1), F32(0)).astype(BF16)
+    total = jnp.zeros((1, 1), F32)
+    meta_ref[...] = jnp.zeros_like(meta_ref)
+    for r in range(rounds):
+        owner = order_ref[r]
+        wanted_ref[r * rows : (r + 1) * rows, :] = shares_ref[owner, :rows, :]
+        counts = jnp.where(mine, shares_ref[owner, rows:, :].astype(F32), 0.0)
+        starts = dot(counts.astype(BF16), before, ((1,), (0,)))[:1] + total
+        counts = counts[:1]
+        total = total + jnp.sum(counts, axis=1, keepdims=True)
+        meta_ref[r : r + 1, :] = starts.astype(jnp.int32)
+        meta_ref[rounds + r : rounds + r + 1, :] = counts.astype(jnp.int32)
+    tail = jnp.where(lane == 0, total.astype(jnp.int32), jnp.where(lane == 1, quarter, 0))
+    meta_ref[2 * rounds : 2 * rounds + 1, :] = tail
+
+
 def per_device(captions, caption_lengths, video_bank, owner_order):
     n_vid, n_tok = lax.axis_size("vid"), lax.axis_size("tok")
     capb, slots, width = captions.shape[1:]
     rounds = owner_order.shape[0]
-    videos = video_bank.shape[0]
     line = n_vid // PAIR
     caps = capb // (n_vid * n_tok)
     rows = caps * slots
-    tok = lax.axis_index("tok")
-    quarter = lax.axis_index("vid") % PAIR * n_tok + tok
     swap_tok = [(0, 1), (1, 0)]
     swap_pair = [(i, i ^ 1) for i in range(n_vid)]
+    swap_both = [
+        (i * n_tok + t, (i ^ 1) * n_tok + (t ^ 1)) for i in range(n_vid) for t in range(n_tok)
+    ]
+    vmem = pl.BlockSpec(memory_space=pltpu.VMEM)
+    small = pltpu.CompilerParams(vmem_limit_bytes=VMEM_BYTES)
 
     tok_bank = lax.ppermute(video_bank, "tok", swap_tok)
     pair_bank = lax.ppermute(video_bank, "vid", swap_pair)
     both_bank = lax.ppermute(tok_bank, "vid", swap_pair)
 
-    mine = lax.dynamic_index_in_dim(
-        captions.reshape(n_vid, n_tok, rows, width), tok, 1, keepdims=False
-    )
-    counts = jnp.pad(caption_lengths.astype(captions.dtype), ((0, COUNT_ROWS - 1), (0, width - capb)))
-    counts = jnp.broadcast_to(counts, (n_vid, COUNT_ROWS, width))
-    pieces = jnp.concatenate([mine, counts], axis=1)
+    pieces = pl.pallas_call(
+        lambda *refs: prepare_kernel("tok", *refs),
+        in_specs=[pl.BlockSpec(memory_space=pltpu.HBM)] * 2,
+        out_specs=pl.BlockSpec(memory_space=pltpu.HBM),
+        out_shape=jax.ShapeDtypeStruct((n_vid, rows + COUNT_ROWS, width), captions.dtype),
+        scratch_shapes=[
+            pltpu.VMEM((n_vid, rows + COUNT_ROWS, width), captions.dtype),
+            pltpu.VMEM(caption_lengths.shape, caption_lengths.dtype),
+            pltpu.SemaphoreType.DMA((n_vid + 1,)),
+            pltpu.SemaphoreType.DMA((n_vid,)),
+        ],
+        name="prepare",
+    )(captions.reshape(n_vid, n_tok, rows, width), caption_lengths)
     shares = lax.all_to_all(pieces, "vid", 0, 0, tiled=True)
-    owners = [owner_order[r] for r in range(rounds)]
-    wanted = jnp.concatenate(
-        [lax.dynamic_index_in_dim(shares, o, 0, keepdims=False)[:rows] for o in owners]
-    )
+    wanted, meta = pl.pallas_call(
+        lambda *refs: pick_kernel(caps, PAIR * n_tok, "vid", "tok", *refs),
+        in_specs=[pl.BlockSpec(memory_space=pltpu.SMEM), vmem],
+        out_specs=[vmem] * 2,
+        out_shape=[
+            jax.ShapeDtypeStruct((rounds * rows, width), captions.dtype),
+            jax.ShapeDtypeStruct((-(-(2 * rounds + 1) // 8) * 8, LANES), jnp.int32),
+        ],
+        compiler_params=small,
+        name="pick",
+    )(owner_order, shares)
     lines = [[k * PAIR + s for k in range(line)] for s in range(PAIR)]
     query = lax.all_gather(wanted, "vid", axis=0, axis_index_groups=lines)
     query = query.reshape(line, rounds, rows, width)
 
-    counts = jnp.concatenate(
-        [lax.dynamic_slice(shares, (o, rows, 0), (1, 1, capb)).reshape(1, capb) for o in owners]
-    ).astype(jnp.int32)
-    lane = jnp.arange(capb, dtype=jnp.int32)
-    counts = jnp.where(lane // caps % (PAIR * n_tok) == quarter, counts, 0)
-    flat = counts.reshape(rounds * capb)
-    place = jnp.arange(rounds * capb, dtype=jnp.int32)
-    starts = jnp.sum(jnp.where(place[None, :] < place[:, None], flat[None, :], 0), axis=1)
-    tail = jnp.where(lane == 0, jnp.sum(flat), jnp.where(lane == 1, quarter, 0))
-    meta = jnp.concatenate([starts.reshape(rounds, capb), counts, tail[None]])
-    meta = jnp.pad(meta, ((0, -meta.shape[0] % 8), (0, 0)))
-
-    scores = pair_scores(slots, caps, meta, query, (video_bank, tok_bank, pair_bank, both_bank))
-    scores = scores[:videos] + lax.ppermute(scores[videos:], "vid", swap_pair)
-    return scores + lax.ppermute(scores, "tok", swap_tok)
+    near, far = pair_scores(slots, caps, meta, query, (video_bank, tok_bank, pair_bank, both_bank))
+    near = near + lax.ppermute(near, "tok", swap_tok)
+    return near + lax.ppermute(far, "vid", swap_pair) + lax.ppermute(far, ("vid", "tok"), swap_both)
 
 
 def solution(mesh):

time: 61.6 us -> 60.7 us (0.985)
  between operations: 5.71 us -> 0.06 us
  waiting for transfers between devices: 9.79 us -> 14.2 us
  other arithmetic: 3.68 us -> 0.62 us
  Pallas kernels: 11.9 us -> 14.5 us
  starting transfers between devices: 11.2 us -> 13.1 us
  local copies, waits for them, and re-layouts: 1.21 us -> 0.01 us
    all_to_all x1, waiting for transfers between devices: 6.37 us -> 11.1 us  [per_device(): shares = lax.all_to_all(pieces, 'vid', 0, 0, tiled=True)]
    pallas_call x0 -> x2, Pallas kernels: none -> 2.53 us  [the longest x1 1.84 us: per_device(): pl.pallas_call(lambda *refs: prepare_kernel('tok', *refs), in_specs=[pl.B...]
    ppermute x1, starting transfers between devices: 0.15 us -> 1.65 us  [per_device(): both_bank = lax.ppermute(tok_bank, 'vid', swap_pair)]
    select_n x2 -> x0, other arithmetic: 1.3 us -> none  [the longest x1 0.65 us: per_device(): tail = jnp.where(lane == 0, jnp.sum(flat), jnp.where(lane == 1, quarter, 0))]
    concatenate x3 -> x0, other arithmetic: 0.87 us -> none  [the longest x1 0.84 us: per_device(): pieces = jnp.concatenate([mine, counts], axis=1)]
    convert_element_type x1 -> x0, other arithmetic: 0.75 us -> none  [per_device(): caption_lengths.astype(captions.dtype)]
    slice x3 -> x0, local copies, waits for them, and re-layouts: 0.64 us -> none  [the longest x1 0.61 us: per_device(): owners = [owner_order[r] for r in range(rounds)]]
    ppermute x2 -> x3, waiting for transfers between devices: 3.41 us -> 3.08 us  [the longest x1 2.04 us: per_device(): lax.ppermute(far, 'vid', swap_pair)]
  transfers between devices with their start and end apart: 6 -> 7, of which waited for: 3 -> 3; matrix products, arithmetic and copies ran while one was open for 3% -> 0% of each run, Pallas kernels for 0% -> 1%
where the time goes in v3:
time: 60.7 us; the launch traced here: 60.2 us
  blocking collectives  17.7 us (29%)
  Pallas kernels  14.5 us (24%)
  waiting for transfers between devices  14.2 us (23%)
  starting transfers between devices  13.1 us (22%)
  other arithmetic  0.62 us (1%)
    all_gather x1, blocking collectives, per_device(): query = lax.all_gather(wanted, 'vid', axis=0, axis_index_groups=lines)  17.7 us
    pallas_call x1, Pallas kernels, pair_scores(): pl.pallas_call(lambda *refs: score_kernel(slots, caps, *refs), in_specs=[...  12 us
    all_to_all x1, waiting for transfers between devices, per_device(): shares = lax.all_to_all(pieces, 'vid', 0, 0, tiled=True)  11.1 us
    all_to_all x1, starting transfers between devices, per_device(): shares = lax.all_to_all(pieces, 'vid', 0, 0, tiled=True)  7.45 us
    ppermute x1, waiting for transfers between devices, per_device(): lax.ppermute(far, 'vid', swap_pair)  2.04 us
    ppermute x1, starting transfers between devices, per_device(): pair_bank = lax.ppermute(video_bank, 'vid', swap_pair)  2.01 us
    pallas_call x1, Pallas kernels, per_device(): pl.pallas_call(lambda *refs: prepare_kernel('tok', *refs), in_specs=[pl.B...  1.84 us
    ppermute x1, starting transfers between devices, per_device(): lax.ppermute(far, 'vid', swap_pair)  1.68 us
  transfers between devices with their start and end apart: 7, of which 3 were waited for; matrix products, arithmetic and copies ran while one was open for 0% of the time, Pallas kernels for 1%

profile of v3, /device:TPU:0, one launch (start us, length us, event | category | flops | bytes accessed | tf_op | source)
XLA Modules:
  0.0 60.2 jit_solution(13185645241023666253)
XLA Ops:
  0.0 1.8 %prepare.1 = bf16[8,264,128]{2,1,0:T(8,128)(2,1)} custom-call(bf16[8,2,256,128]{3,2,1,0:T(8,128)(2,1)} %bitcast.3, s32[1,128]{1,0:T(1,128)} %refs_1_.1), custom_call_target="tpu_custom_call" | custom-call | tf_op jit(solution)/shard_map/prepare/pallas_call | solution.py:210
  1.9 0.0 copy-start
  1.9 0.0 copy-start.1
  1.9 7.5 %all-to-all-start = ((bf16[8,264,128]{2,1,0:T(8,128)(2,1)}), bf16[8,264,128]{2,1,0:T(8,128)(2,1)S(1)}, u32[]{:S(2)}, u32[]{:S(2)}) async-start(bf16[8,264,128]{2,1,0:T(8,128)(2,1)} %prepare.1), calls=%async_computation | async-start | bytes 1081344 | tf_op jit(solution)/shard_map/all_to_all | solution.py:223
  9.3 0.0 copy-done
  9.3 0.1 collective-permute-start
  9.4 2.0 %collective-permute-start.1 = (bf16[12,128,128]{2,1,0:T(8,128)(2,1)S(1)}, bf16[12,128,128]{2,1,0:T(8,128)(2,1)S(1)}, u32[]{:S(2)}, u32[]{:S(2)}) collective-permute-start(bf16[12,128,128]{2,1,0:T(8,128)(2,1)S(1)} %copy-done), channel_id=1, source_target_pairs={{0,2},{2,0},{4,6},{6,4},{8,10},{10,8},{12,14},{14,12},{1,3},{3,1},... | collective-permute-start | bytes 1179656 | tf_op jit(solution)/shard_map/ppermute | solution.py:207
  11.4 0.0 collective-permute-done.refs_4_
  11.4 1.6 %collective-permute-start.2 = (bf16[12,128,128]{2,1,0:T(8,128)(2,1)S(1)}, bf16[12,128,128]{2,1,0:T(8,128)(2,1)S(1)}, u32[]{:S(2)}, u32[]{:S(2)}) collective-permute-start(bf16[12,128,128]{2,1,0:T(8,128)(2,1)S(1)} %collective-permute-done.refs_4_), channel_id=1, source_target_pairs={{0,2},{2,0},{4,6},{6,4},{8,10},{10,8},{12,14},{14,12},{1,3},{3,1},... | collective-permute-start | bytes 1179656 | tf_op jit(solution)/shard_map/ppermute | solution.py:208
  13.1 11.1 %all-to-all-done.refs_1_ = bf16[8,264,128]{2,1,0:T(8,128)(2,1)S(1)} async-done(((bf16[8,264,128]{2,1,0:T(8,128)(2,1)}), bf16[8,264,128]{2,1,0:T(8,128)(2,1)S(1)}, u32[]{:S(2)}, u32[]{:S(2)}) %all-to-all-start) | async-done | bytes 540704 | tf_op jit(solution)/shard_map/all_to_all | solution.py:223
  24.2 0.0 copy-done.1
  24.2 0.7 %pick.1 = (bf16[768,128]{1,0:T(8,128)(2,1)S(1)}, s32[8,128]{1,0:T(8,128)S(1)}) custom-call(s32[3]{0:T(128)S(1)} %copy-done.1, bf16[8,264,128]{2,1,0:T(8,128)(2,1)S(1)} %all-to-all-done.refs_1_), custom_call_target="tpu_custom_call" | custom-call | tf_op jit(solution)/shard_map/pick/pallas_call | solution.py:224
  24.9 17.7 %all-gather = bf16[3072,128]{1,0:T(8,128)(2,1)S(1)} all-gather(bf16[768,128]{1,0:T(8,128)(2,1)S(1)} %get-tuple-element.10), channel_id=2, replica_groups={{0,4,8,12},{2,6,10,14},{1,5,9,13},{3,7,11,15},{16,20,24,28},{18,22,26,3..., dimensions={0}, use_global_device_ids=true | all-gather | bytes 983040 | tf_op jit(solution)/shard_map/all_gather | solution.py:236
  42.6 0.0 collective-permute-done.1.refs_5_
  42.6 0.0 collective-permute-done.2.refs_6_
  42.6 12.0 %soft_scores.1 = (f32[12,384]{1,0:T(8,128)S(1)}, f32[12,384]{1,0:T(8,128)S(1)}) custom-call(s32[8,128]{1,0:T(8,128)S(1)} %get-tuple-element.9.refs_0_.refs_1_, s32[8,128]{1,0:T(8,128)S(1)} %get-tuple-element.9.refs_0_.refs_1_, bf16[4,3,256,128]{3,2,1,0:T(8,128)(2,1)S(1)} %bitcast.2, bf16[12,128,128]{2,1,0:T(8,128)(2,1)S(1)} %copy-done, ...), custom_call_target="tpu_custom_call" | custom-call | tf_op jit(solution)/shard_map/soft_scores/pallas_call | solution.py:123
  54.6 0.1 collective-permute-start.3
  54.7 1.7 %collective-permute-start.4 = (f32[12,384]{1,0:T(8,128)S(1)}, f32[12,384]{1,0:T(8,128)S(1)}, u32[]{:S(2)}, u32[]{:S(2)}) collective-permute-start(f32[12,384]{1,0:T(8,128)S(1)} %get-tuple-element.12), channel_id=1, source_target_pairs={{0,2},{2,0},{4,6},{6,4},{8,10},{10,8},{12,14},{14,12},{1,3},{3,1},... | collective-permute-start | bytes 55304 | tf_op jit(solution)/shard_map/ppermute | solution.py:241
  56.4 0.2 collective-permute-start.5
  56.5 0.0 collective-permute-done.3
  56.5 2.0 %collective-permute-done.4 = f32[12,384]{1,0:T(8,128)S(1)} collective-permute-done((f32[12,384]{1,0:T(8,128)S(1)}, f32[12,384]{1,0:T(8,128)S(1)}, u32[]{:S(2)}, u32[]{:S(2)}) %collective-permute-start.4) | collective-permute-done | bytes 18464 | tf_op jit(solution)/shard_map/ppermute | solution.py:241
  58.6 1.0 %collective-permute-done.5 = f32[12,384]{1,0:T(8,128)S(1)} collective-permute-done((f32[12,384]{1,0:T(8,128)S(1)}, f32[12,384]{1,0:T(8,128)S(1)}, u32[]{:S(2)}, u32[]{:S(2)}) %collective-permute-start.5) | collective-permute-done | bytes 18464 | tf_op jit(solution)/shard_map/ppermute | solution.py:241
  59.6 0.6 %add_add_fusion = f32[12,384]{1,0:T(8,128)} fusion(f32[12,384]{1,0:T(8,128)S(1)} %collective-permute-done.5, f32[12,384]{1,0:T(8,128)S(1)} %collective-permute-done.4, f32[12,384]{1,0:T(8,128)S(1)} %get-tuple-element.11, f32[12,384]{1,0:T(8,128)S(1)} %collective-permute-done.3), kind=kLoop, calls=%fused_computation | loop fusion | flops 13824 | bytes 92160 | tf_op jit(solution)/shard_map/add | solution.py:241
Async XLA Ops:
  1.9 7.5 %copy-start = (bf16[12,128,128]{2,1,0:T(8,128)(2,1)S(1)}, bf16[12,128,128]{2,1,0:T(8,128)(2,1)}, u32[]{:S(2)}) copy-start(bf16[12,128,128]{2,1,0:T(8,128)(2,1)} %refs_3_.1) | copy-start | bytes 1179652
  1.9 22.3 %copy-start.1 = (s32[3]{0:T(128)S(1)}, s32[3]{0:T(128)}, u32[]{:S(2)}) copy-start(s32[3]{0:T(128)} %refs_0_.1) | copy-start | bytes 40
  1.9 22.3 %all-to-all-start = ((bf16[8,264,128]{2,1,0:T(8,128)(2,1)}), bf16[8,264,128]{2,1,0:T(8,128)(2,1)S(1)}, u32[]{:S(2)}, u32[]{:S(2)}) async-start(bf16[8,264,128]{2,1,0:T(8,128)(2,1)} %prepare.1), calls=%async_computation | async-start | bytes 1081344 | tf_op jit(solution)/shard_map/all_to_all | solution.py:223
  9.3 2.1 %collective-permute-start = (bf16[12,128,128]{2,1,0:T(8,128)(2,1)S(1)}, bf16[12,128,128]{2,1,0:T(8,128)(2,1)S(1)}, u32[]{:S(2)}, u32[]{:S(2)}) collective-permute-start(bf16[12,128,128]{2,1,0:T(8,128)(2,1)S(1)} %copy-done), channel_id=1, source_target_pairs={{0,1},{1,0},{2,3},{3,2},{4,5},{5,4},{6,7},{7,6},{8,9},{9,8},{10,11... | collective-permute-start | bytes 1179656 | tf_op jit(solution)/shard_map/ppermute | solution.py:206
  9.4 33.2 %collective-permute-start.1 = (bf16[12,128,128]{2,1,0:T(8,128)(2,1)S(1)}, bf16[12,128,128]{2,1,0:T(8,128)(2,1)S(1)}, u32[]{:S(2)}, u32[]{:S(2)}) collective-permute-start(bf16[12,128,128]{2,1,0:T(8,128)(2,1)S(1)} %copy-done), channel_id=1, source_target_pairs={{0,2},{2,0},{4,6},{6,4},{8,10},{10,8},{12,14},{14,12},{1,3},{3,1},... | collective-permute-start | bytes 1179656 | tf_op jit(solution)/shard_map/ppermute | solution.py:207
  11.4 31.2 %collective-permute-start.2 = (bf16[12,128,128]{2,1,0:T(8,128)(2,1)S(1)}, bf16[12,128,128]{2,1,0:T(8,128)(2,1)S(1)}, u32[]{:S(2)}, u32[]{:S(2)}) collective-permute-start(bf16[12,128,128]{2,1,0:T(8,128)(2,1)S(1)} %collective-permute-done.refs_4_), channel_id=1, source_target_pairs={{0,2},{2,0},{4,6},{6,4},{8,10},{10,8},{12,14},{14,12},{1,3},{3,1},... | collective-permute-start | bytes 1179656 | tf_op jit(solution)/shard_map/ppermute | solution.py:208
  54.6 1.9 %collective-permute-start.3 = (f32[12,384]{1,0:T(8,128)S(1)}, f32[12,384]{1,0:T(8,128)S(1)}, u32[]{:S(2)}, u32[]{:S(2)}) collective-permute-start(f32[12,384]{1,0:T(8,128)S(1)} %get-tuple-element.11), channel_id=1, source_target_pairs={{0,1},{1,0},{2,3},{3,2},{4,5},{5,4},{6,7},{7,6},{8,9},{9,8},{10,11... | collective-permute-start | bytes 55304 | tf_op jit(solution)/shard_map/ppermute | solution.py:240
  54.7 3.9 %collective-permute-start.4 = (f32[12,384]{1,0:T(8,128)S(1)}, f32[12,384]{1,0:T(8,128)S(1)}, u32[]{:S(2)}, u32[]{:S(2)}) collective-permute-start(f32[12,384]{1,0:T(8,128)S(1)} %get-tuple-element.12), channel_id=1, source_target_pairs={{0,2},{2,0},{4,6},{6,4},{8,10},{10,8},{12,14},{14,12},{1,3},{3,1},... | collective-permute-start | bytes 55304 | tf_op jit(solution)/shard_map/ppermute | solution.py:241
  56.4 3.3 %collective-permute-start.5 = (f32[12,384]{1,0:T(8,128)S(1)}, f32[12,384]{1,0:T(8,128)S(1)}, u32[]{:S(2)}, u32[]{:S(2)}) collective-permute-start(f32[12,384]{1,0:T(8,128)S(1)} %get-tuple-element.12), channel_id=1, source_target_pairs={{0,3},{1,2},{2,1},{3,0},{4,7},{5,6},{6,5},{7,4},{8,11},{9,10},{10,... | collective-permute-start | bytes 55304 | tf_op jit(solution)/shard_map/ppermute | solution.py:241

commit v4 on v3

--- a/solution.py
+++ b/solution.py
@@ -10,6 +10,7 @@
 LN2 = 0.6931471805599453
 COUNT_ROWS = 8
 PAIR = 2
+STEPS = 4
 TILE = 256
 LANES = 128
 JOBS = 2
@@ -22,34 +23,22 @@
     return lax.dot_general(a, b, (dims, ((), ())), preferred_element_type=F32)
 
 
-def score_kernel(slots, caps, meta_ref, lanes_ref, q_hbm, own_ref, tok_ref, pair_ref, both_ref,
-                 near_ref, far_ref, q_ref, bank_ref, out_ref, rows_ref,
-                 soft_ref, a_ref, b_ref, sems):
-    line, rounds = q_ref.shape[:2]
-    quarters = LANES // (line * caps)
-    videos, half = own_ref.shape[:2]
-    tokens = 2 * half
-    fetch_q = pltpu.make_async_copy(q_hbm, q_ref, sems.at[0])
-    fetch_q.start()
-    banks = []
-    for k, src in enumerate((own_ref, tok_ref, pair_ref, both_ref)):
-        dst = bank_ref.at[pl.ds(k // 2 * videos, videos), pl.ds(k % 2 * half, half), :]
-        banks.append(pltpu.make_async_copy(src, dst, sems.at[1 + k]))
-        banks[-1].start()
-    fetch_q.wait()
-    total_rows, quarter = meta_ref[2 * rounds, 0], meta_ref[2 * rounds, 1]
+def score_kernel(slots, caps, meta_ref, lanes_ref, q_ref, bank_ref, *refs):
+    past, refs = refs[:-7], refs[-7:]
+    near_ref, far_ref, out_ref, rows_ref, soft_ref, a_ref, b_ref = refs
+    blocks, rounds = q_ref.shape[:2]
+    videos, tokens = bank_ref.shape[0] // 2, bank_ref.shape[1]
+    total_rows, first_cap, stride = (meta_ref[2 * rounds, k] for k in range(3))
 
     def pack(i, carry):
-        r, g = i // line, i % line
+        r, g = i // blocks, i % blocks
         piece = q_ref[g, r].astype(F32)
         for c in range(caps):
-            start = meta_ref[r, (g * quarters + quarter) * caps + c]
+            start = meta_ref[r, first_cap + g * stride + c]
             rows_ref[pl.ds(start, slots), :] = piece[c * slots : (c + 1) * slots]
         return carry
 
-    lax.fori_loop(0, rounds * line, pack, 0)
-    for copy in banks:
-        copy.wait()
+    lax.fori_loop(0, rounds * blocks, pack, 0)
     out_ref[...] = jnp.zeros_like(out_ref)
     scale = F32(SHARPNESS * LOG2E)
     per = 2 * videos // JOBS
@@ -110,34 +99,48 @@
     for r in range(rounds):
         count = jnp.maximum(lanes_ref[rounds + r : rounds + r + 1, :], 1).astype(F32)
         mean = out_ref[:, r * LANES : (r + 1) * LANES] / count
-        near_ref[:, r * LANES : (r + 1) * LANES] = mean[:videos]
-        far_ref[:, r * LANES : (r + 1) * LANES] = mean[videos:]
-
-
-def pair_scores(slots, caps, meta, query, banks):
-    line, rounds, rows, width = query.shape
-    videos, half = banks[0].shape[:2]
-    n_rows = -(-(rounds * line * rows) // TILE) * TILE + TILE + slots
+        for k, ref in enumerate((near_ref, far_ref)):
+            part = mean[k * videos : (k + 1) * videos]
+            if past:
+                part = part + past[k][:, r * LANES : (r + 1) * LANES]
+            ref[:, r * LANES : (r + 1) * LANES] = part
+
+
+def share_scores(slots, caps, meta, query, bank, *past):
+    blocks, rounds, rows, width = query.shape
+    videos, tokens = bank.shape[0] // 2, bank.shape[1]
+    n_rows = -(-(rounds * blocks * rows) // TILE) * TILE + TILE + slots
     vmem = pl.BlockSpec(memory_space=pltpu.VMEM)
-    anywhere = pl.BlockSpec(memory_space=pl.ANY)
+    work = 2 * videos * tokens * rounds * blocks * rows
     return pl.pallas_call(
         lambda *refs: score_kernel(slots, caps, *refs),
-        in_specs=[pl.BlockSpec(memory_space=pltpu.SMEM), vmem] + [anywhere] * 5,
+        in_specs=[pl.BlockSpec(memory_space=pltpu.SMEM)] + [vmem] * (3 + len(past)),
         out_specs=[vmem] * 2,
         out_shape=[jax.ShapeDtypeStruct((videos, rounds * LANES), F32)] * 2,
         scratch_shapes=[
-            pltpu.VMEM(query.shape, query.dtype),
-            pltpu.VMEM((2 * videos, 2 * half, width), banks[0].dtype),
             pltpu.VMEM((2 * videos, rounds * LANES), F32),
             pltpu.VMEM((n_rows, width), F32),
             pltpu.VMEM((2, 2 * videos, TILE), F32),
-            pltpu.VMEM((2 * videos // JOBS * 2 * half, TILE), F32),
-            pltpu.VMEM((2 * videos // JOBS * 2 * half, TILE), F32),
-            pltpu.SemaphoreType.DMA((5,)),
+            pltpu.VMEM((2 * videos // JOBS * tokens, TILE), F32),
+            pltpu.VMEM((2 * videos // JOBS * tokens, TILE), F32),
         ],
         compiler_params=pltpu.CompilerParams(vmem_limit_bytes=VMEM_BYTES),
+        cost_estimate=pl.CostEstimate(
+            flops=4 * work * width, transcendentals=work, bytes_accessed=bank.size * 2
+        ),
         name="soft_scores",
-    )(meta, meta, query, *banks)
+    )(meta, meta, query, bank, *past)
+
+
+def merge_kernel(own_ref, tok_ref, pair_ref, both_ref, _, out_ref, sems):
+    videos, half = own_ref.shape[:2]
+    moves = []
+    for k, src in enumerate((own_ref, tok_ref, pair_ref, both_ref)):
+        dst = out_ref.at[pl.ds(k // 2 * videos, videos), pl.ds(k % 2 * half, half), :]
+        moves.append(pltpu.make_async_copy(src, dst, sems.at[k]))
+        moves[-1].start()
+    for move in moves:
+        move.wait()
 
 
 def prepare_kernel(tok_axis, block_ref, counts_ref, out_ref, piece_ref, count_ref, in_sems, out_sems):
@@ -163,35 +166,44 @@
         move.wait()
 
 
-def pick_kernel(caps, quarters, vid_axis, tok_axis, order_ref, shares_ref, wanted_ref, meta_ref):
+def pick_kernel(caps, quarters, inner, vid_axis, tok_axis, order_ref, shares_ref, wanted_ref, *metas):
     rounds = order_ref.shape[0]
     rows = shares_ref.shape[1] - COUNT_ROWS
-    quarter = lax.axis_index(vid_axis) % PAIR * (quarters // PAIR) + lax.axis_index(tok_axis)
+    vid = lax.axis_index(vid_axis)
+    quarter = vid % PAIR * (quarters // PAIR) + lax.axis_index(tok_axis)
+    place = vid // PAIR % inner
     lane = lax.broadcasted_iota(jnp.int32, (1, LANES), 1)
-    mine = lane // caps % quarters == quarter
     before = lax.broadcasted_iota(jnp.int32, (LANES, LANES), 0) < lax.broadcasted_iota(
         jnp.int32, (LANES, LANES), 1
     )
     before = jnp.where(before, F32(1), F32(0)).astype(BF16)
-    total = jnp.zeros((1, 1), F32)
-    meta_ref[...] = jnp.zeros_like(meta_ref)
+    counts = []
     for r in range(rounds):
         owner = order_ref[r]
         wanted_ref[r * rows : (r + 1) * rows, :] = shares_ref[owner, :rows, :]
-        counts = jnp.where(mine, shares_ref[owner, rows:, :].astype(F32), 0.0)
-        starts = dot(counts.astype(BF16), before, ((1,), (0,)))[:1] + total
-        counts = counts[:1]
-        total = total + jnp.sum(counts, axis=1, keepdims=True)
-        meta_ref[r : r + 1, :] = starts.astype(jnp.int32)
-        meta_ref[rounds + r : rounds + r + 1, :] = counts.astype(jnp.int32)
-    tail = jnp.where(lane == 0, total.astype(jnp.int32), jnp.where(lane == 1, quarter, 0))
-    meta_ref[2 * rounds : 2 * rounds + 1, :] = tail
+        counts.append(shares_ref[owner, rows:, :].astype(F32))
+    for k, meta_ref in enumerate(metas):
+        block = (place ^ k) * quarters + quarter
+        mine = lane // caps % (inner * quarters) == block
+        kept = [jnp.where(mine, count, 0.0) for count in counts]
+        starts = dot(jnp.concatenate(kept, axis=0).astype(BF16), before, ((1,), (0,)))
+        total = jnp.zeros((1, 1), F32)
+        meta_ref[...] = jnp.zeros_like(meta_ref)
+        for r in range(rounds):
+            begin = starts[r * COUNT_ROWS : r * COUNT_ROWS + 1] + total
+            total = total + jnp.sum(kept[r][:1], axis=1, keepdims=True)
+            meta_ref[r : r + 1, :] = begin.astype(jnp.int32)
+            meta_ref[rounds + r : rounds + r + 1, :] = kept[r][:1].astype(jnp.int32)
+        tail = jnp.where(lane == 1, block * caps, jnp.where(lane == 2, inner * quarters * caps, 0))
+        tail = jnp.where(lane == 0, total.astype(jnp.int32), tail)
+        meta_ref[2 * rounds : 2 * rounds + 1, :] = tail
 
 
 def per_device(captions, caption_lengths, video_bank, owner_order):
     n_vid, n_tok = lax.axis_size("vid"), lax.axis_size("tok")
     capb, slots, width = captions.shape[1:]
     rounds = owner_order.shape[0]
+    videos, half = video_bank.shape[:2]
     line = n_vid // PAIR
     caps = capb // (n_vid * n_tok)
     rows = caps * slots
@@ -221,22 +233,41 @@
         name="prepare",
     )(captions.reshape(n_vid, n_tok, rows, width), caption_lengths)
     shares = lax.all_to_all(pieces, "vid", 0, 0, tiled=True)
-    wanted, meta = pl.pallas_call(
-        lambda *refs: pick_kernel(caps, PAIR * n_tok, "vid", "tok", *refs),
+    inner = min(STEPS, line)
+    wanted, *metas = pl.pallas_call(
+        lambda *refs: pick_kernel(caps, PAIR * n_tok, inner, "vid", "tok", *refs),
         in_specs=[pl.BlockSpec(memory_space=pltpu.SMEM), vmem],
-        out_specs=[vmem] * 2,
-        out_shape=[
-            jax.ShapeDtypeStruct((rounds * rows, width), captions.dtype),
-            jax.ShapeDtypeStruct((-(-(2 * rounds + 1) // 8) * 8, LANES), jnp.int32),
-        ],
+        out_specs=[vmem] * (1 + inner),
+        out_shape=[jax.ShapeDtypeStruct((rounds * rows, width), captions.dtype)]
+        + [jax.ShapeDtypeStruct((-(-(2 * rounds + 1) // 8) * 8, LANES), jnp.int32)] * inner,
         compiler_params=small,
         name="pick",
     )(owner_order, shares)
-    lines = [[k * PAIR + s for k in range(line)] for s in range(PAIR)]
-    query = lax.all_gather(wanted, "vid", axis=0, axis_index_groups=lines)
-    query = query.reshape(line, rounds, rows, width)
-
-    near, far = pair_scores(slots, caps, meta, query, (video_bank, tok_bank, pair_bank, both_bank))
+    blocks = line // inner
+    if blocks > 1:
+        groups = [
+            [(b * inner + m) * PAIR + s for b in range(blocks)] for m in range(inner) for s in range(PAIR)
+        ]
+        wanted = lax.all_gather(wanted, "vid", axis=0, axis_index_groups=groups)
+    wanted = wanted.reshape(blocks, rounds, rows, width)
+    arrived = [wanted]
+    for k in range(1, inner):
+        steps = [(i, i ^ (k * PAIR)) for i in range(n_vid)]
+        arrived.append(lax.ppermute(wanted, "vid", steps))
+
+    bank = pl.pallas_call(
+        merge_kernel,
+        in_specs=[pl.BlockSpec(memory_space=pl.ANY)] * 5,
+        out_specs=vmem,
+        out_shape=jax.ShapeDtypeStruct((2 * videos, 2 * half, width), video_bank.dtype),
+        scratch_shapes=[pltpu.SemaphoreType.DMA((4,))],
+        compiler_params=small,
+        name="merge",
+    )(video_bank, tok_bank, pair_bank, both_bank, metas[0])
+    scores = ()
+    for meta, query in zip(metas, arrived):
+        scores = share_scores(slots, caps, meta, query, bank, *scores)
+    near, far = scores
     near = near + lax.ppermute(near, "tok", swap_tok)
     return near + lax.ppermute(far, "vid", swap_pair) + lax.ppermute(far, ("vid", "tok"), swap_both)
 

time: 60.7 us -> 57.5 us (0.947)
  blocking collectives: 17.7 us -> 0 us
  Pallas kernels: 14.5 us -> 20.7 us
  waiting for transfers between devices: 14.2 us -> 18.5 us
  starting transfers between devices: 13.1 us -> 17.4 us
    all_gather x1 -> x0, blocking collectives: 17.7 us -> none  [per_device(): query = lax.all_gather(wanted, 'vid', axis=0, axis_index_groups=lines)]
    pallas_call x2 -> x6, Pallas kernels: 12.7 us -> 18.8 us  [the longest x4 17.9 us: share_scores(): pl.pallas_call(lambda *refs: score_kernel(slots, caps, *refs), in_specs=[...]
    ppermute x1, waiting for transfers between devices: 0.01 us -> 5.31 us  [per_device(): both_bank = lax.ppermute(tok_bank, 'vid', swap_pair)]
    ppermute x0 -> x3, starting transfers between devices: none -> 4.45 us  [per_device(): arrived.append(lax.ppermute(wanted, 'vid', steps))]
    ppermute x1, starting transfers between devices: 1.68 us -> 0.46 us  [per_device(): lax.ppermute(far, 'vid', swap_pair)]
    ppermute x1, starting transfers between devices: 0.17 us -> 1.39 us  [per_device(): lax.ppermute(far, ('vid', 'tok'), swap_both)]
    ppermute x1, waiting for transfers between devices: 1.04 us -> 0.01 us  [per_device(): lax.ppermute(far, ('vid', 'tok'), swap_both)]
  transfers between devices with their start and end apart: 7 -> 10, of which waited for: 3 -> 3; matrix products, arithmetic and copies ran while one was open for 0% -> 0% of each run, Pallas kernels for 1% -> 25%
where the time goes in v4:
time: 57.5 us; the launch traced here: 57.3 us
  Pallas kernels  20.7 us (36%)
  waiting for transfers between devices  18.5 us (32%)
  starting transfers between devices  17.4 us (30%)
  other arithmetic  0.62 us (1%)
    pallas_call x4, Pallas kernels, share_scores(): pl.pallas_call(lambda *refs: score_kernel(slots, caps, *refs), in_specs=[...  17.9 us
    all_to_all x1, waiting for transfers between devices, per_device(): shares = lax.all_to_all(pieces, 'vid', 0, 0, tiled=True)  11.1 us
    all_to_all x1, starting transfers between devices, per_device(): shares = lax.all_to_all(pieces, 'vid', 0, 0, tiled=True)  7.32 us
    ppermute x1, waiting for transfers between devices, per_device(): both_bank = lax.ppermute(tok_bank, 'vid', swap_pair)  5.31 us
    ppermute x3, starting transfers between devices, per_device(): arrived.append(lax.ppermute(wanted, 'vid', steps))  4.45 us
    ppermute x1, waiting for transfers between devices, per_device(): lax.ppermute(far, 'vid', swap_pair)  2.12 us
    ppermute x1, starting transfers between devices, per_device(): pair_bank = lax.ppermute(video_bank, 'vid', swap_pair)  2.01 us
    pallas_call x1, Pallas kernels, per_device(): pl.pallas_call(lambda *refs: prepare_kernel('tok', *refs), in_specs=[pl.B...  1.89 us
  transfers between devices with their start and end apart: 10, of which 3 were waited for; matrix products, arithmetic and copies ran while one was open for 0% of the time, Pallas kernels for 25%

profile of v4, /device:TPU:0, one launch (start us, length us, event | category | flops | bytes accessed | tf_op | source)
XLA Modules:
  0.0 57.3 jit_solution(11854573232880447399)
XLA Ops:
  0.0 0.0 copy-start
  0.0 0.0 copy-start.1
  0.0 1.9 %prepare.1 = bf16[8,264,128]{2,1,0:T(8,128)(2,1)} custom-call(bf16[8,2,256,128]{3,2,1,0:T(8,128)(2,1)} %bitcast.6, s32[1,128]{1,0:T(1,128)} %refs_1_.1), custom_call_target="tpu_custom_call" | custom-call | tf_op jit(solution)/shard_map/prepare/pallas_call | solution.py:222
  1.9 7.3 %all-to-all-start = ((bf16[8,264,128]{2,1,0:T(8,128)(2,1)}), bf16[8,264,128]{2,1,0:T(8,128)(2,1)S(1)}, u32[]{:S(2)}, u32[]{:S(2)}) async-start(bf16[8,264,128]{2,1,0:T(8,128)(2,1)} %prepare.1), calls=%async_computation | async-start | bytes 1081344 | tf_op jit(solution)/shard_map/all_to_all | solution.py:235
  9.2 0.0 copy-done
  9.2 0.1 collective-permute-start.1
  9.3 2.0 %collective-permute-start.2 = (bf16[12,128,128]{2,1,0:T(8,128)(2,1)S(1)}, bf16[12,128,128]{2,1,0:T(8,128)(2,1)S(1)}, u32[]{:S(2)}, u32[]{:S(2)}) collective-permute-start(bf16[12,128,128]{2,1,0:T(8,128)(2,1)S(1)} %copy-done), channel_id=1, source_target_pairs={{0,2},{2,0},{4,6},{6,4},{8,10},{10,8},{12,14},{14,12},{1,3},{3,1},... | collective-permute-start | bytes 1179656 | tf_op jit(solution)/shard_map/ppermute | solution.py:219
  11.3 0.0 collective-permute-done.1.tok_ref
  11.3 1.6 %collective-permute-start.3 = (bf16[12,128,128]{2,1,0:T(8,128)(2,1)S(1)}, bf16[12,128,128]{2,1,0:T(8,128)(2,1)S(1)}, u32[]{:S(2)}, u32[]{:S(2)}) collective-permute-start(bf16[12,128,128]{2,1,0:T(8,128)(2,1)S(1)} %collective-permute-done.1.tok_ref), channel_id=1, source_target_pairs={{0,2},{2,0},{4,6},{6,4},{8,10},{10,8},{12,14},{14,12},{1,3},{3,1},... | collective-permute-start | bytes 1179656 | tf_op jit(solution)/shard_map/ppermute | solution.py:220
  13.0 11.1 %all-to-all-done.refs_1_ = bf16[8,264,128]{2,1,0:T(8,128)(2,1)S(1)} async-done(((bf16[8,264,128]{2,1,0:T(8,128)(2,1)}), bf16[8,264,128]{2,1,0:T(8,128)(2,1)S(1)}, u32[]{:S(2)}, u32[]{:S(2)}) %all-to-all-start) | async-done | bytes 540704 | tf_op jit(solution)/shard_map/all_to_all | solution.py:235
  24.1 0.0 copy-done.1
  24.1 0.7 %pick.1 = (bf16[768,128]{1,0:T(8,128)(2,1)S(1)}, s32[8,128]{1,0:T(8,128)S(1)}, s32[8,128]{1,0:T(8,128)S(1)}, s32[8,128]{1,0:T(8,128)S(1)}, s32[8,128]{1,0:T(8,128)S(1)}) custom-call(s32[3]{0:T(128)S(1)} %copy-done.1, bf16[8,264,128]{2,1,0:T(8,128)(2,1)S(1)} %all-to-all-done.refs_1_), custom_call_target="tpu_custom_call" | custom-call | tf_op jit(solution)/shard_map/pick/pallas_call | solution.py:237
  24.8 0.9 %collective-permute-start.5 = (bf16[1,3,256,128]{3,2,1,0:T(8,128)(2,1)S(1)}, bf16[1,3,256,128]{3,2,1,0:T(8,128)(2,1)S(1)}, u32[]{:S(2)}, u32[]{:S(2)}) collective-permute-start(bf16[1,3,256,128]{3,2,1,0:T(8,128)(2,1)S(1)} %bitcast.2), channel_id=1, source_target_pairs={{0,4},{2,6},{4,0},{6,2},{8,12},{10,14},{12,8},{14,10},{1,5},{3,7},... | collective-permute-start | bytes 589832 | tf_op jit(solution)/shard_map/ppermute | solution.py:256
  25.7 0.9 %collective-permute-start.4 = (bf16[1,3,256,128]{3,2,1,0:T(8,128)(2,1)S(1)}, bf16[1,3,256,128]{3,2,1,0:T(8,128)(2,1)S(1)}, u32[]{:S(2)}, u32[]{:S(2)}) collective-permute-start(bf16[1,3,256,128]{3,2,1,0:T(8,128)(2,1)S(1)} %bitcast.3), channel_id=1, source_target_pairs={{0,8},{2,10},{4,12},{6,14},{8,0},{10,2},{12,4},{14,6},{1,9},{3,11}... | collective-permute-start | bytes 589832 | tf_op jit(solution)/shard_map/ppermute | solution.py:256
  26.6 2.6 %collective-permute-start = (bf16[1,3,256,128]{3,2,1,0:T(8,128)(2,1)S(1)}, bf16[1,3,256,128]{3,2,1,0:T(8,128)(2,1)S(1)}, u32[]{:S(2)}, u32[]{:S(2)}) collective-permute-start(bf16[1,3,256,128]{3,2,1,0:T(8,128)(2,1)S(1)} %bitcast.4), channel_id=1, source_target_pairs={{0,12},{2,14},{4,8},{6,10},{8,4},{10,6},{12,0},{14,2},{1,13},{3,15... | collective-permute-start | bytes 589832 | tf_op jit(solution)/shard_map/ppermute | solution.py:256
  29.2 0.0 collective-permute-done.2.pair_ref
  29.2 5.3 %collective-permute-done.3.both_ref = bf16[12,128,128]{2,1,0:T(8,128)(2,1)S(1)} collective-permute-done((bf16[12,128,128]{2,1,0:T(8,128)(2,1)S(1)}, bf16[12,128,128]{2,1,0:T(8,128)(2,1)S(1)}, u32[]{:S(2)}, u32[]{:S(2)}) %collective-permute-start.3) | collective-permute-done | bytes 393248 | tf_op jit(solution)/shard_map/ppermute | solution.py:220
  34.5 0.1 merge.1.refs_3_
  34.7 4.5 %soft_scores.4 = (f32[12,384]{1,0:T(8,128)S(1)}, f32[12,384]{1,0:T(8,128)S(1)}) custom-call(s32[8,128]{1,0:T(8,128)S(1)} %get-tuple-element.20._.refs_0_.refs_1_, s32[8,128]{1,0:T(8,128)S(1)} %get-tuple-element.20._.refs_0_.refs_1_, bf16[1,3,256,128]{3,2,1,0:T(8,128)(2,1)S(1)} %bitcast.5, bf16[24,256,128]{2,1,0:T(8,128)(2,1)S(1)} %merge.1.refs_3_), custom_call_target="tpu_custom_call" | custom-call | flops 2415919104 | bytes 1572864 | tf_op jit(solution)/shard_map/soft_scores/pallas_call | solution.py:115
  39.2 0.0 collective-permute-done.5.refs_2_
  39.2 4.5 %soft_scores.5 = (f32[12,384]{1,0:T(8,128)S(1)}, f32[12,384]{1,0:T(8,128)S(1)}) custom-call(s32[8,128]{1,0:T(8,128)S(1)} %get-tuple-element.22.refs_0_.refs_1_, s32[8,128]{1,0:T(8,128)S(1)} %get-tuple-element.22.refs_0_.refs_1_, bf16[1,3,256,128]{3,2,1,0:T(8,128)(2,1)S(1)} %collective-permute-done.5.refs_2_, bf16[24,256,128]{2,1,0:T(8,128)(2,1)S(1)} %merge.1.refs_3_, ...), custom_call_target="tpu_custom_call" | custom-call | flops 2415919104 | bytes 1572864 | tf_op jit(solution)/shard_map/soft_scores/pallas_call | solution.py:115
  43.7 0.0 collective-permute-done.4.refs_2_
  43.7 4.5 %soft_scores.6 = (f32[12,384]{1,0:T(8,128)S(1)}, f32[12,384]{1,0:T(8,128)S(1)}) custom-call(s32[8,128]{1,0:T(8,128)S(1)} %get-tuple-element.21.refs_0_.refs_1_, s32[8,128]{1,0:T(8,128)S(1)} %get-tuple-element.21.refs_0_.refs_1_, bf16[1,3,256,128]{3,2,1,0:T(8,128)(2,1)S(1)} %collective-permute-done.4.refs_2_, bf16[24,256,128]{2,1,0:T(8,128)(2,1)S(1)} %merge.1.refs_3_, ...), custom_call_target="tpu_custom_call" | custom-call | flops 2415919104 | bytes 1572864 | tf_op jit(solution)/shard_map/soft_scores/pallas_call | solution.py:115
  48.2 0.0 collective-permute-done.refs_2_
  48.2 4.5 %soft_scores.7 = (f32[12,384]{1,0:T(8,128)S(1)}, f32[12,384]{1,0:T(8,128)S(1)}) custom-call(s32[8,128]{1,0:T(8,128)S(1)} %get-tuple-element.18.refs_0_.refs_1_, s32[8,128]{1,0:T(8,128)S(1)} %get-tuple-element.18.refs_0_.refs_1_, bf16[1,3,256,128]{3,2,1,0:T(8,128)(2,1)S(1)} %collective-permute-done.refs_2_, bf16[24,256,128]{2,1,0:T(8,128)(2,1)S(1)} %merge.1.refs_3_, ...), custom_call_target="tpu_custom_call" | custom-call | flops 2415919104 | bytes 1572864 | tf_op jit(solution)/shard_map/soft_scores/pallas_call | solution.py:115
  52.7 0.1 collective-permute-start.6
  52.7 0.5 collective-permute-start.7
  53.2 1.4 %collective-permute-start.8 = (f32[12,384]{1,0:T(8,128)S(1)}, f32[12,384]{1,0:T(8,128)S(1)}, u32[]{:S(2)}, u32[]{:S(2)}) collective-permute-start(f32[12,384]{1,0:T(8,128)S(1)} %get-tuple-element.30), channel_id=1, source_target_pairs={{0,3},{1,2},{2,1},{3,0},{4,7},{5,6},{6,5},{7,4},{8,11},{9,10},{10,... | collective-permute-start | bytes 55304 | tf_op jit(solution)/shard_map/ppermute | solution.py:272
  54.6 0.0 collective-permute-done.6
  54.6 2.1 %collective-permute-done.7 = f32[12,384]{1,0:T(8,128)S(1)} collective-permute-done((f32[12,384]{1,0:T(8,128)S(1)}, f32[12,384]{1,0:T(8,128)S(1)}, u32[]{:S(2)}, u32[]{:S(2)}) %collective-permute-start.7) | collective-permute-done | bytes 18464 | tf_op jit(solution)/shard_map/ppermute | solution.py:272
  56.7 0.0 collective-permute-done.8
  56.7 0.6 %add_add_fusion = f32[12,384]{1,0:T(8,128)} fusion(f32[12,384]{1,0:T(8,128)S(1)} %collective-permute-done.8, f32[12,384]{1,0:T(8,128)S(1)} %collective-permute-done.7, f32[12,384]{1,0:T(8,128)S(1)} %get-tuple-element.29, f32[12,384]{1,0:T(8,128)S(1)} %collective-permute-done.6), kind=kLoop, calls=%fused_computation | loop fusion | flops 13824 | bytes 92160 | tf_op jit(solution)/shard_map/add | solution.py:272
Async XLA Ops:
  0.0 9.2 %copy-start = (bf16[12,128,128]{2,1,0:T(8,128)(2,1)S(1)}, bf16[12,128,128]{2,1,0:T(8,128)(2,1)}, u32[]{:S(2)}) copy-start(bf16[12,128,128]{2,1,0:T(8,128)(2,1)} %own_ref.1) | copy-start | bytes 1179652
  0.0 24.1 %copy-start.1 = (s32[3]{0:T(128)S(1)}, s32[3]{0:T(128)}, u32[]{:S(2)}) copy-start(s32[3]{0:T(128)} %refs_0_.1) | copy-start | bytes 40
  1.9 22.2 %all-to-all-start = ((bf16[8,264,128]{2,1,0:T(8,128)(2,1)}), bf16[8,264,128]{2,1,0:T(8,128)(2,1)S(1)}, u32[]{:S(2)}, u32[]{:S(2)}) async-start(bf16[8,264,128]{2,1,0:T(8,128)(2,1)} %prepare.1), calls=%async_computation | async-start | bytes 1081344 | tf_op jit(solution)/shard_map/all_to_all | solution.py:235
  9.2 2.1 %collective-permute-start.1 = (bf16[12,128,128]{2,1,0:T(8,128)(2,1)S(1)}, bf16[12,128,128]{2,1,0:T(8,128)(2,1)S(1)}, u32[]{:S(2)}, u32[]{:S(2)}) collective-permute-start(bf16[12,128,128]{2,1,0:T(8,128)(2,1)S(1)} %copy-done), channel_id=1, source_target_pairs={{0,1},{1,0},{2,3},{3,2},{4,5},{5,4},{6,7},{7,6},{8,9},{9,8},{10,11... | collective-permute-start | bytes 1179656 | tf_op jit(solution)/shard_map/ppermute | solution.py:218
  9.3 19.9 %collective-permute-start.2 = (bf16[12,128,128]{2,1,0:T(8,128)(2,1)S(1)}, bf16[12,128,128]{2,1,0:T(8,128)(2,1)S(1)}, u32[]{:S(2)}, u32[]{:S(2)}) collective-permute-start(bf16[12,128,128]{2,1,0:T(8,128)(2,1)S(1)} %copy-done), channel_id=1, source_target_pairs={{0,2},{2,0},{4,6},{6,4},{8,10},{10,8},{12,14},{14,12},{1,3},{3,1},... | collective-permute-start | bytes 1179656 | tf_op jit(solution)/shard_map/ppermute | solution.py:219
  11.3 23.2 %collective-permute-start.3 = (bf16[12,128,128]{2,1,0:T(8,128)(2,1)S(1)}, bf16[12,128,128]{2,1,0:T(8,128)(2,1)S(1)}, u32[]{:S(2)}, u32[]{:S(2)}) collective-permute-start(bf16[12,128,128]{2,1,0:T(8,128)(2,1)S(1)} %collective-permute-done.1.tok_ref), channel_id=1, source_target_pairs={{0,2},{2,0},{4,6},{6,4},{8,10},{10,8},{12,14},{14,12},{1,3},{3,1},... | collective-permute-start | bytes 1179656 | tf_op jit(solution)/shard_map/ppermute | solution.py:220
  24.8 14.4 %collective-permute-start.5 = (bf16[1,3,256,128]{3,2,1,0:T(8,128)(2,1)S(1)}, bf16[1,3,256,128]{3,2,1,0:T(8,128)(2,1)S(1)}, u32[]{:S(2)}, u32[]{:S(2)}) collective-permute-start(bf16[1,3,256,128]{3,2,1,0:T(8,128)(2,1)S(1)} %bitcast.2), channel_id=1, source_target_pairs={{0,4},{2,6},{4,0},{6,2},{8,12},{10,14},{12,8},{14,10},{1,5},{3,7},... | collective-permute-start | bytes 589832 | tf_op jit(solution)/shard_map/ppermute | solution.py:256
  25.7 18.0 %collective-permute-start.4 = (bf16[1,3,256,128]{3,2,1,0:T(8,128)(2,1)S(1)}, bf16[1,3,256,128]{3,2,1,0:T(8,128)(2,1)S(1)}, u32[]{:S(2)}, u32[]{:S(2)}) collective-permute-start(bf16[1,3,256,128]{3,2,1,0:T(8,128)(2,1)S(1)} %bitcast.3), channel_id=1, source_target_pairs={{0,8},{2,10},{4,12},{6,14},{8,0},{10,2},{12,4},{14,6},{1,9},{3,11}... | collective-permute-start | bytes 589832 | tf_op jit(solution)/shard_map/ppermute | solution.py:256
  26.6 21.6 %collective-permute-start = (bf16[1,3,256,128]{3,2,1,0:T(8,128)(2,1)S(1)}, bf16[1,3,256,128]{3,2,1,0:T(8,128)(2,1)S(1)}, u32[]{:S(2)}, u32[]{:S(2)}) collective-permute-start(bf16[1,3,256,128]{3,2,1,0:T(8,128)(2,1)S(1)} %bitcast.4), channel_id=1, source_target_pairs={{0,12},{2,14},{4,8},{6,10},{8,4},{10,6},{12,0},{14,2},{1,13},{3,15... | collective-permute-start | bytes 589832 | tf_op jit(solution)/shard_map/ppermute | solution.py:256
  52.7 1.9 %collective-permute-start.6 = (f32[12,384]{1,0:T(8,128)S(1)}, f32[12,384]{1,0:T(8,128)S(1)}, u32[]{:S(2)}, u32[]{:S(2)}) collective-permute-start(f32[12,384]{1,0:T(8,128)S(1)} %get-tuple-element.29), channel_id=1, source_target_pairs={{0,1},{1,0},{2,3},{3,2},{4,5},{5,4},{6,7},{7,6},{8,9},{9,8},{10,11... | collective-permute-start | bytes 55304 | tf_op jit(solution)/shard_map/ppermute | solution.py:271
  52.7 4.0 %collective-permute-start.7 = (f32[12,384]{1,0:T(8,128)S(1)}, f32[12,384]{1,0:T(8,128)S(1)}, u32[]{:S(2)}, u32[]{:S(2)}) collective-permute-start(f32[12,384]{1,0:T(8,128)S(1)} %get-tuple-element.30), channel_id=1, source_target_pairs={{0,2},{2,0},{4,6},{6,4},{8,10},{10,8},{12,14},{14,12},{1,3},{3,1},... | collective-permute-start | bytes 55304 | tf_op jit(solution)/shard_map/ppermute | solution.py:272
  53.2 3.5 %collective-permute-start.8 = (f32[12,384]{1,0:T(8,128)S(1)}, f32[12,384]{1,0:T(8,128)S(1)}, u32[]{:S(2)}, u32[]{:S(2)}) collective-permute-start(f32[12,384]{1,0:T(8,128)S(1)} %get-tuple-element.30), channel_id=1, source_target_pairs={{0,3},{1,2},{2,1},{3,0},{4,7},{5,6},{6,5},{7,4},{8,11},{9,10},{10,... | collective-permute-start | bytes 55304 | tf_op jit(solution)/shard_map/ppermute | solution.py:272
